TPU v7x, 512 devices: a whole 4x4x16 slice. The times are simulated.
512 devices in a mesh: lat: 128 (over x, z, core), chan: 4 (over y).
Axes of the slice: x: 4, y: 4, z: 16, core: 2. Of those that a mesh axis runs over, the one named last changes fastest.
Arguments:
- grid: bfloat16 [384, 720, 512], P('lat', None, 'chan'), may hold values from -6 to 6
- basis: float32 [384, 384, 384], P('lat'), may hold values from -16 to 16, as said below
- mix_weight: bfloat16 [2, 512, 512], P(None, None, 'chan'), may hold values from -0.1875 to 0.1875
- spectral_gain: float32 [384], replicated, may hold values from 0.5 to 4
- conv_weight: float32 [9, 512], P(None, 'chan'), may hold values from -2 to 2
- lat_offsets: int32 [9], replicated, may hold values from -1 to 1
- lon_offsets: int32 [9], replicated, may hold values from -3 to 3
- ln_gain: float32 [512], replicated, may hold values from 0.1 to 1.9
- up_weight: bfloat16 [512, 512], replicated, may hold values from -0.25 to 0.25
- down_weight: bfloat16 [512, 512], replicated, may hold values from -0.25 to 0.25
Outputs:
- result: bfloat16 [384, 720, 512], P('lat', None, 'chan')
Inputs may be any that keep to these rules, and one draw needn't show every extreme that they name: basis[m, l, t] is the orthonormal associated Legendre function of degree l and order m at cos(theta_t) times a factor between 0.8 and 1.25; it is zero for l < m.
All inputs are finite; a program needn't handle non-finite values.
Results may differ from a plain program's by a relative error of at most 0.01.
Values may be sent and summed in bfloat16 or wider, within the bound.
A program may use at most 64 MiB of HBM per device.

v0:
```python
import math

import jax
import jax.numpy as jnp
from jax import lax
from jax.sharding import Mesh
from jax.sharding import PartitionSpec as P

MMAX = 384
L = 384
LAT = ("lat_0", "lat_1", "lat_2")


def in_order(blocks, dim):
    lengths = list(blocks.shape[1:])
    lengths[dim] *= blocks.shape[0]
    return jnp.moveaxis(blocks, 0, dim).reshape(lengths)


def copy_for_each(value, axis):
    copies = jnp.broadcast_to(value, (lax.axis_size(axis), *value.shape))
    return lax.all_to_all(copies, axis, split_axis=0, concat_axis=0, tiled=True)


def gathered_copies(value, axis, dim):
    return in_order(copy_for_each(value, axis), dim)


def in_blocks(value, dim, length):
    before, after = (value.shape[:dim], value.shape[dim + 1 :])
    return jnp.moveaxis(value.reshape(*before, length, -1, *after), dim, 0)


def exchange_in_order(blocks, axes, turns):
    lengths = [lax.axis_size(a) for a in axes]
    blocks = blocks.reshape(*lengths, *blocks.shape[1:])
    for k in turns:
        blocks = lax.all_to_all(blocks, axes[k], split_axis=k, concat_axis=k, tiled=True)
    return blocks.reshape(-1, *blocks.shape[len(axes) :])


def exchange_by_chip(value, groups, turns, split_dim, concat_dim):
    length = lax.axis_size(groups[0]) * lax.axis_size(groups[1])
    blocks = in_blocks(value, split_dim, length)
    return in_order(exchange_in_order(blocks, groups, turns), concat_dim)


def padded_2(value, sides, width):
    for axis, dim in sides:
        size, length = (lax.axis_size(axis), value.shape[dim])
        up = [(i, (i + 1) % size) for i in range(size - 1)]
        down = [(j, i) for i, j in up]
        last = lax.slice_in_dim(value, length - width, length, axis=dim)
        first = lax.slice_in_dim(value, 0, width, axis=dim)
        before = lax.ppermute(last, axis, up)
        after = lax.ppermute(first, axis, down)
        value = jnp.concatenate([before, value, after], axis=dim)
    return value


def cycle_angle(rows, nlat):
    return math.pi * (rows.astype(jnp.float32) + 0.5) / nlat


def complex_mix(real_in, imag_in, real_w, imag_w):
    real_out = jnp.dot(real_in, real_w, preferred_element_type=jnp.float32) - jnp.dot(
        imag_in, imag_w, preferred_element_type=jnp.float32
    )
    imag_out = jnp.dot(real_in, imag_w, preferred_element_type=jnp.float32) + jnp.dot(
        imag_in, real_w, preferred_element_type=jnp.float32
    )
    return (real_out, imag_out)


def on_device(
    grid,
    basis,
    mix_weight,
    spectral_gain,
    conv_weight,
    lat_offsets,
    lon_offsets,
    ln_gain,
    up_weight,
    down_weight,
):
    cycles, nlon, width = grid.shape
    groups = lax.axis_size(LAT)
    rank = lax.axis_index(LAT)
    nlat = cycles * groups
    modes = basis.shape[0]
    points = jnp.arange(nlon, dtype=jnp.int32)
    all_orders = jnp.arange(MMAX, dtype=jnp.int32)
    phase = points[:, None] * all_orders[None, :] % nlon
    angle = 2.0 * math.pi * phase.astype(jnp.float32) / nlon
    fwd_table = (
        jnp.stack([jnp.cos(angle), -jnp.sin(angle)], axis=-1)
        .reshape(nlon, 2 * MMAX)
        .astype(jnp.bfloat16)
    )
    weight_m = jnp.where(all_orders == 0, 1.0, 2.0).astype(jnp.float32)[None, :]
    inv_table = (
        jnp.stack([weight_m * jnp.cos(angle), -weight_m * jnp.sin(angle)], axis=-1)
        .reshape(nlon, 2 * MMAX)
        .T.astype(jnp.bfloat16)
    )
    spec = jnp.einsum("tpc,pk->tkc", grid, fwd_table, preferred_element_type=jnp.float32) * (
        1.0 / nlon
    )
    spec = spec.astype(jnp.bfloat16).reshape(cycles, groups, modes, 2, width)
    gathered = lax.all_to_all(spec, LAT, split_axis=1, concat_axis=0, tiled=True).reshape(
        nlat, modes, 2 * width
    )
    theta = cycle_angle(jnp.arange(nlat, dtype=jnp.int32), nlat)
    quad = math.pi / nlat * jnp.sin(theta)
    fwd_leg = (basis * quad[None, None, :]).astype(jnp.bfloat16)
    inv_leg = basis.astype(jnp.bfloat16)
    coeff = jnp.einsum(
        "jlt,tjk->jlk", fwd_leg, gathered, preferred_element_type=jnp.float32
    ).astype(jnp.bfloat16)
    coeff = coeff.reshape(modes, L, 2, width)
    piece = gathered_copies(coeff, "chan", 3)
    count = piece.shape[3]
    real_w = mix_weight[0]
    imag_w = mix_weight[1]
    real_out, imag_out = complex_mix(
        piece[:, :, 0, :].reshape(-1, count), piece[:, :, 1, :].reshape(-1, count), real_w, imag_w
    )
    summed_modes = jnp.concatenate([real_out, imag_out], axis=1)
    mixed = (summed_modes.reshape(modes, L, 2 * width) * spectral_gain[None, :, None]).astype(
        jnp.bfloat16
    )
    back = jnp.einsum("jlt,jlk->tjk", inv_leg, mixed, preferred_element_type=jnp.float32).astype(
        jnp.bfloat16
    )
    back = exchange_by_chip(
        back.reshape(nlat, 1, modes, 2, width), (("lat_0", "lat_1"), "lat_2"), (1, 0), 0, 1
    )
    back = back.reshape(cycles, 2 * MMAX, width)
    spectral = jnp.einsum("tkc,kp->tpc", back, inv_table, preferred_element_type=jnp.float32)
    padded = padded_2(grid, ((LAT, 0),), 1)
    own_cycles = rank * cycles + jnp.arange(cycles, dtype=jnp.int32)
    here = jnp.sin(cycle_angle(own_cycles, nlat))
    local = jnp.zeros((cycles, nlon, width), jnp.float32)
    for tap in range(conv_weight.shape[0]):
        shift = lat_offsets[tap]
        source = lax.dynamic_slice_in_dim(padded, 1 + shift, cycles, 0)
        source = jnp.roll(source, -lon_offsets[tap], axis=1)
        ratio = (jnp.sin(cycle_angle(own_cycles + shift, nlat)) / here)[:, None, None]
        local = local + conv_weight[tap][None, None, :] * ratio * source.astype(jnp.float32)
    summed = (spectral + local + grid.astype(jnp.float32)).astype(jnp.bfloat16)
    block = lax.all_to_all(summed, "chan", split_axis=1, concat_axis=2, tiled=True)
    count, span, channels = block.shape
    rows = block.reshape(-1, channels).astype(jnp.float32)
    center = jnp.mean(rows, axis=-1, keepdims=True)
    spread = jnp.mean((rows - center) ** 2, axis=-1, keepdims=True)
    normed = ((rows - center) / jnp.sqrt(spread + 1e-05) * ln_gain).astype(jnp.bfloat16)
    hidden = jax.nn.gelu(
        jnp.dot(normed, up_weight, preferred_element_type=jnp.float32), approximate=True
    ).astype(jnp.bfloat16)
    output = (jnp.dot(hidden, down_weight, preferred_element_type=jnp.float32) + rows).astype(
        jnp.bfloat16
    )
    return lax.all_to_all(
        output.reshape(count, span, channels), "chan", split_axis=2, concat_axis=1, tiled=True
    )


def solution(mesh):
    finer = Mesh(
        mesh.devices.reshape(4, 16, 2, mesh.shape["chan"]), ("lat_0", "lat_1", "lat_2", "chan")
    )
    return jax.shard_map(
        on_device,
        mesh=finer,
        in_specs=(
            P(LAT, None, "chan"),
            P(LAT, None, None),
            P(None, None, "chan"),
            P(),
            P(None, "chan"),
            P(),
            P(),
            P(),
            P(),
            P(),
        ),
        out_specs=P(LAT, None, "chan"),
        check_vma=False,
    )
```

profile of v0, /device:TPU:32, one launch (start us, length us, event | category | flops | bytes accessed | tf_op | source)
XLA Modules:
  0.0 209.3 jit_solution(5487940598081768799)
XLA Ops:
  0.0 4.9 %negate_convert_fusion = (bf16[720,384,1]{1,0,2:T(8,128)(2,1)S(1)}, bf16[720,384,1]{1,0,2:T(8,128)(2,1)S(1)}) fusion(), kind=kLoop, calls=%fused_computation.52 | loop fusion | flops 3317760 | bytes 1105920 | tf_op jit(solution)/shard_map/convert.6
  5.0 1.8 copy.81
  6.8 1.0 convert_element_type.226
  7.9 0.8 fusion.2
  8.7 1.2 copy.83
  9.9 19.1 %all-to-all-start = ((bf16[3,128,3,2,128]{4,3,0,2,1:T(2,128)(2,1)}), bf16[3,128,3,2,128]{4,3,0,2,1:T(2,128)(2,1)S(1)}, u32[]{:S(2)}, u32[]{:S(2)}) async-start(bf16[3,128,3,2,128]{4,3,0,2,1:T(2,128)(2,1)} %copy.83), calls=%async_computation | async-start | bytes 1179648 | tf_op jit(solution)/shard_map/all_to_all | solution.py:111
  29.0 0.8 fusion.59
  29.8 2.0 collective-permute-start
  31.8 3.5 %collective-permute-start.1 = (bf16[1,720,128]{2,1,0:T(8,128)(2,1)}, bf16[1,720,128]{2,1,0:T(8,128)(2,1)}, u32[]{:S(2)}, u32[]{:S(2)}) collective-permute-start(bf16[1,720,128]{2,1,0:T(8,128)(2,1)} %get-tuple-element.17), channel_id=1, source_target_pairs={{4,0},{8,4},{12,8},{16,12},{20,16},{24,20},{28,24},{32,28},{36,32}... | collective-permute-start | bytes 552968 | tf_op jit(solution)/shard_map/ppermute | solution.py:56
  35.5 0.7 fusion.60
  36.1 30.2 %all-to-all-done = bf16[3,128,3,2,128]{4,3,0,2,1:T(2,128)(2,1)S(1)} async-done(((bf16[3,128,3,2,128]{4,3,0,2,1:T(2,128)(2,1)}), bf16[3,128,3,2,128]{4,3,0,2,1:T(2,128)(2,1)S(1)}, u32[]{:S(2)}, u32[]{:S(2)}) %all-to-all-start) | async-done | bytes 589856 | tf_op jit(solution)/shard_map/all_to_all | solution.py:111
  66.3 0.4 copy.84
  66.7 0.4 reshape.566
  67.1 0.7 copy-done.1
  67.8 0.6 convolution_convert_fusion.1
  68.4 1.8 broadcast_in_dim.12
  70.2 4.6 %all-to-all-start.1 = ((bf16[4,3,384,2,128]{2,4,3,1,0:T(8,128)(2,1)}), bf16[4,3,384,2,128]{2,4,3,1,0:T(8,128)(2,1)S(1)}, u32[]{:S(2)}, u32[]{:S(2)}) async-start(bf16[4,3,384,2,128]{2,4,3,1,0:T(8,128)(2,1)} %broadcast_in_dim.12), calls=%async_computation.1 | async-start | bytes 4718592 | tf_op jit(solution)/shard_map/all_to_all | solution.py:22
  74.8 1.3 sine_divide_fusion
  76.1 1.3 sine_divide_fusion.2
  77.4 1.3 sine_divide_fusion.4
  78.7 0.7 fusion.61
  79.4 4.5 %multiply_convert_fusion.3 = bf16[720,384,1]{1,0,2:T(8,128)(2,1)S(1)} fusion(f32[384]{0:T(512)S(1)} %get-tuple-element.49), kind=kLoop, calls=%fused_computation.53 | loop fusion | flops 3041280 | bytes 554496 | tf_op jit(solution)/shard_map/convert.8
  83.9 4.5 %multiply_convert_fusion.4 = bf16[720,384,1]{1,0,2:T(8,128)(2,1)S(1)} fusion(f32[384]{0:T(512)S(1)} %get-tuple-element.48), kind=kLoop, calls=%fused_computation.54 | loop fusion | flops 3041280 | bytes 554496 | tf_op jit(solution)/shard_map/convert.7
  88.4 1.1 pad_maximum_fusion.1
  89.7 12.4 %all-to-all-done.1 = bf16[4,3,384,2,128]{2,4,3,1,0:T(8,128)(2,1)S(1)} async-done(((bf16[4,3,384,2,128]{2,4,3,1,0:T(8,128)(2,1)}), bf16[4,3,384,2,128]{2,4,3,1,0:T(8,128)(2,1)S(1)}, u32[]{:S(2)}, u32[]{:S(2)}) %all-to-all-start.1) | async-done | bytes 2359328 | tf_op jit(solution)/shard_map/all_to_all | solution.py:22
  102.2 0.3 copy.86
  102.5 1.3 fusion.58
  103.7 1.6 copy.87
  105.4 1.3 fusion.42
  106.7 0.5 fusion.46
  107.2 0.6 copy.88
  107.9 1.7 convolution_add_fusion
  109.5 0.5 convolution_subtract_fusion
  110.0 1.1 pad_maximum_fusion
  111.1 1.8 copy.89
  113.0 1.5 fusion.5
  114.4 1.3 copy.91
  115.9 0.4 copy.92
  116.3 4.2 %all_to_all.57 = bf16[64,2,3,1,3,2,128]{6,5,2,0,4,3,1:T(2,128)(2,1)S(1)} all-to-all(bf16[64,2,3,1,3,2,128]{6,5,2,0,4,3,1:T(2,128)(2,1)S(1)} %copy.92), channel_id=1, replica_groups=mesh['lat_0'=4,'lat_1'=16,'lat_2'=2,'chan'=4] {'lat_2'}, dimensions={1} | all-to-all | bytes 1179648 | tf_op jit(solution)/shard_map/all_to_all | solution.py:38
  120.5 1.2 copy.93
  121.7 6.7 %all-to-all-start.3 = ((bf16[64,2,3,1,3,2,128]{6,5,2,1,4,3,0:T(2,128)(2,1)}), bf16[64,2,3,1,3,2,128]{6,5,2,1,4,3,0:T(2,128)(2,1)S(1)}, u32[]{:S(2)}, u32[]{:S(2)}) async-start(bf16[64,2,3,1,3,2,128]{6,5,2,1,4,3,0:T(2,128)(2,1)} %copy.93), calls=%async_computation.3 | async-start | bytes 1179648 | tf_op jit(solution)/shard_map/all_to_all | solution.py:38
  128.5 0.7 sine_divide_fusion.8
  146.3 1.8 copy.80
  148.1 1.8 convert_element_type.223
  149.9 1.4 sine_divide_fusion.6
  151.7 0.9 constant_dynamic-update-slice_fusion.2
  152.8 0.9 constant_dynamic-update-slice_fusion
  153.7 2.1 %constant_dynamic-slice_fusion.8 = (bf16[3,720,128]{2,1,0:T(8,128)(2,1)S(1)}, bf16[3,720,128]{2,1,0:T(8,128)(2,1)}, bf16[3,720,128]{2,1,0:T(8,128)(2,1)}, bf16[3...) fusion(bf16[5,720,128]{2,1,0:T(8,128)(2,1)S(1)} %constant_dynam, ...), kind=kLoop, calls=%fused_computation.101 | loop fusion | bytes 9953316 | tf_op jit(solution)/shard_map/dynamic_slice | solution.py:147
  155.9 6.6 %all-to-all-done.3 = bf16[64,2,3,1,3,2,128]{6,5,2,1,4,3,0:T(2,128)(2,1)S(1)} async-done(((bf16[64,2,3,1,3,2,128]{6,5,2,1,4,3,0:T(2,128)(2,1)}), bf16[64,2,3,1,3,2,128]{6,5,2,1,4,3,0:T(2,128)(2,1)S(1)}, u32[]{:S(2)}, u32[]{:S(2)}) %all-to-all-start.3) | async-done | bytes 589856 | tf_op jit(solution)/shard_map/all_to_all | solution.py:38
  162.4 0.6 copy.94
  163.0 0.6 copy.95
  163.7 8.7 %fusion.4 = bf16[3,720,128]{2,1,0:T(8,128)(2,1)S(1)} fusion(bf16[3,768,128]{2,1,0:T(8,128)(2,1)S(1)} %bitcast.121, bf16[720,768]{0,1:T(8,128)(2,1)S(1)} %copy-done.6, bf16[3,720,128]{2,1,0:T(8,128)(2,1)S(1)} %copy-done.5, s32[]{:T(128)S(6)} %select_n.125, bf16[3,720,128]{2,1,0:T(8,128)(2,1)S(1)} %copy-done.10, s32[]{:T(128)S(6)} %select_n.123, ...), kind=kOutput, calls=%fused_computation.14 | convolution fusion | flops 440432640 | bytes 7792164 | tf_op jit(solution)/shard_map/tkc,kp->tpc/dot_general | solution.py:140
  172.4 0.3 copy.97
  172.7 14.2 %all_to_all.58 = bf16[3,720,128]{2,0,1:T(4,128)(2,1)S(1)} all-to-all(bf16[3,720,128]{2,0,1:T(4,128)(2,1)S(1)} %copy.97), channel_id=1, replica_groups=mesh['lat_0'=4,'lat_1'=16,'lat_2'=2,'chan'=4] {'chan'}, dimensions={1} | all-to-all | bytes 1105920 | tf_op jit(solution)/shard_map/all_to_all | solution.py:152
  187.1 0.2 bitcast_reduce_fusion
  187.3 0.3 multiply_reduce_fusion
  187.7 0.3 copy.99
  188.0 0.2 pad.24
  188.4 0.8 copy-done.16
  189.2 1.0 fusion.3
  190.3 0.7 copy.100
  191.0 16.7 %all_to_all.59 = bf16[3,180,512]{1,0,2:T(4,128)(2,1)S(1)} all-to-all(bf16[3,180,512]{1,0,2:T(4,128)(2,1)S(1)} %copy.100), channel_id=1, replica_groups=mesh['lat_0'=4,'lat_1'=16,'lat_2'=2,'chan'=4] {'chan'}, dimensions={2} | all-to-all | bytes 1105920 | tf_op jit(solution)/shard_map/all_to_all | solution.py:164
  207.7 0.7 copy.102
  208.4 0.9 all_to_all.50
  (59 shorter events, 1.7 us)
Async XLA Ops:
  0.0 188.4 %copy-start = (bf16[512,512]{1,0:T(8,128)(2,1)S(1)}, bf16[512,512]{1,0:T(8,128)(2,1)}, u32[]{:S(2)}) copy-start(bf16[512,512]{1,0:T(8,128)(2,1)} %param.21) | copy-start | bytes 1572868
  6.8 1.1 copy-start.4
  9.9 25.5 %copy-start.12 = (s32[9]{0:T(128)S(1)}, s32[9]{0:T(128)}, u32[]{:S(2)}) copy-start(s32[9]{0:T(128)} %param.17) | copy-start | bytes 112
  9.9 56.4 %all-to-all-start = ((bf16[3,128,3,2,128]{4,3,0,2,1:T(2,128)(2,1)}), bf16[3,128,3,2,128]{4,3,0,2,1:T(2,128)(2,1)S(1)}, u32[]{:S(2)}, u32[]{:S(2)}) async-start(bf16[3,128,3,2,128]{4,3,0,2,1:T(2,128)(2,1)} %copy.83), calls=%async_computation | async-start | bytes 1179648 | tf_op jit(solution)/shard_map/all_to_all | solution.py:111
  29.8 121.9 %collective-permute-start = (bf16[1,720,128]{2,1,0:T(8,128)(2,1)}, bf16[1,720,128]{2,1,0:T(8,128)(2,1)}, u32[]{:S(2)}, u32[]{:S(2)}) collective-permute-start(bf16[1,720,128]{2,1,0:T(8,128)(2,1)} %get-tuple-element.18), channel_id=1, source_target_pairs={{0,4},{4,8},{8,12},{12,16},{16,20},{20,24},{24,28},{28,32},{32,36}... | collective-permute-start | bytes 552968 | tf_op jit(solution)/shard_map/ppermute | solution.py:55
  31.8 120.9 %collective-permute-start.1 = (bf16[1,720,128]{2,1,0:T(8,128)(2,1)}, bf16[1,720,128]{2,1,0:T(8,128)(2,1)}, u32[]{:S(2)}, u32[]{:S(2)}) collective-permute-start(bf16[1,720,128]{2,1,0:T(8,128)(2,1)} %get-tuple-element.17), channel_id=1, source_target_pairs={{4,0},{8,4},{12,8},{16,12},{20,16},{24,20},{28,24},{32,28},{36,32}... | collective-permute-start | bytes 552968 | tf_op jit(solution)/shard_map/ppermute | solution.py:56
  66.3 1.5 copy-start.1
  70.2 8.6 %copy-start.13 = (s32[9]{0:T(128)S(1)}, s32[9]{0:T(128)}, u32[]{:S(2)}) copy-start(s32[9]{0:T(128)} %param.18) | copy-start | bytes 112
  70.2 32.0 %all-to-all-start.1 = ((bf16[4,3,384,2,128]{2,4,3,1,0:T(8,128)(2,1)}), bf16[4,3,384,2,128]{2,4,3,1,0:T(8,128)(2,1)S(1)}, u32[]{:S(2)}, u32[]{:S(2)}) async-start(bf16[4,3,384,2,128]{2,4,3,1,0:T(8,128)(2,1)} %broadcast_in_dim.12), calls=%async_computation.1 | async-start | bytes 4718592 | tf_op jit(solution)/shard_map/all_to_all | solution.py:22
  88.4 1.1 copy-start.14
  103.7 1.6 copy-start.7
  105.3 1.3 copy-start.8
  107.8 1.7 copy-start.9
  111.1 1.8 copy-start.2
  111.1 1.8 copy-start.15
  120.5 25.7 %copy-start.3 = (bf16[720,384,2]{1,0,2:T(8,128)(2,1)S(1)}, bf16[720,384,2]{1,0,2:T(8,128)(2,1)}, u32[]{:S(2)}) copy-start(bf16[720,384,2]{1,0,2:T(8,128)(2,1)} %pad_maximum_fusion.1) | copy-start | bytes 3317764
  121.7 40.7 %all-to-all-start.3 = ((bf16[64,2,3,1,3,2,128]{6,5,2,1,4,3,0:T(2,128)(2,1)}), bf16[64,2,3,1,3,2,128]{6,5,2,1,4,3,0:T(2,128)(2,1)S(1)}, u32[]{:S(2)}, u32[]{:S(2)}) async-start(bf16[64,2,3,1,3,2,128]{6,5,2,1,4,3,0:T(2,128)(2,1)} %copy.93), calls=%async_computation.3 | async-start | bytes 1179648 | tf_op jit(solution)/shard_map/all_to_all | solution.py:38
  148.1 4.6 %copy-start.5 = (bf16[3,720,128]{2,1,0:T(8,128)(2,1)S(1)}, bf16[3,720,128]{2,1,0:T(8,128)(2,1)}, u32[]{:S(2)}) copy-start(bf16[3,720,128]{2,1,0:T(8,128)(2,1)} %param.12) | copy-start | bytes 1658884
  155.9 7.8 %copy-start.6 = (bf16[720,768]{0,1:T(8,128)(2,1)S(1)}, bf16[720,768]{0,1:T(8,128)(2,1)}, u32[]{:S(2)}) copy-start(bf16[720,768]{0,1:T(8,128)(2,1)} %convert_element_type.223) | copy-start | bytes 3317764
  162.4 1.2 copy-start.10
  162.4 1.2 copy-start.11
  188.2 1.0 copy-start.16
  188.2 1.0 copy-start.17
where the time goes:
time: 210 us; the launch traced here: 209 us
  waiting for transfers between devices  49.2 us (23%)
  starting transfers between devices  36 us (17%)
  blocking collectives  35.2 us (17%)
  local copies, waits for them, and re-layouts  31.4 us (15%)
  other arithmetic  23.4 us (11%)
  between operations  17.6 us (8%)
  matrix products  16.6 us (8%)
    all_to_all x1, waiting for transfers between devices, on_device(): lax.all_to_all(spec, LAT, split_axis=1, concat_axis=0, tiled=True)  30.2 us
    all_to_all x1, starting transfers between devices, on_device(): lax.all_to_all(spec, LAT, split_axis=1, concat_axis=0, tiled=True)  19.1 us
    all_to_all x1, blocking collectives, on_device(): lax.all_to_all(output.reshape(count, span, channels), 'chan', split_axis=...  16.7 us
    all_to_all x1, blocking collectives, on_device(): lax.all_to_all(summed, 'chan', split_axis=1, concat_axis=2, tiled=True)  14.2 us
    another operation x3, other arithmetic  13.9 us
    all_to_all x1, waiting for transfers between devices, copy_for_each(): return lax.all_to_all(copies, axis, split_axis=0, concat_axis=0, tiled=True)  12.4 us
    dot_general x1, matrix products, on_device(): jnp.einsum('tkc,kp->tpc', back, inv_table, preferred_element_type=jnp.flo...  8.74 us
    all_to_all x1, starting transfers between devices, exchange_in_order(): lax.all_to_all(blocks, axes[k], split_axis=k, concat_axis=k, tiled=True)  6.72 us
  transfers between devices with their start and end apart: 5, of which 3 were waited for; matrix products, arithmetic and copies ran while one was open for 21% of the time, Pallas kernels for 0%

commit v1 on v0

v1 whole, which is shorter than its diff:
```python
import functools
import math

import jax
import jax.numpy as jnp
import ml_dtypes
import numpy as np
from jax import lax
from jax.experimental import pallas as pl
from jax.experimental.pallas import tpu as pltpu
from jax.sharding import Mesh
from jax.sharding import PartitionSpec as P

LAT = ("lat_0", "lat_1", "lat_2")
MESH_ID = pl.DeviceIdType.MESH
TILE = 16
F32 = jnp.float32
BF16 = jnp.bfloat16


def transform_tables(X, Z, K, modes, nlon):
    z, ri, x, k, j = np.meshgrid(
        np.arange(Z), np.arange(2), np.arange(X), np.arange(K), np.arange(modes), indexing="ij"
    )
    m = (((x * Z + z) * K + k) * modes + j).reshape(-1).astype(np.int64)
    part = ri.reshape(-1)
    points = np.arange(nlon, dtype=np.int64)
    phase = (m[:, None] * points[None, :]) % nlon
    angle = np.float32(2.0 * math.pi) * phase.astype(np.float32) / np.float32(nlon)
    table = np.where(part[:, None] == 0, np.cos(angle), -np.sin(angle)).astype(np.float32)
    return table.astype(ml_dtypes.bfloat16)


def cycle_order(X, Z, K, cycles):
    c, x, k, z = np.meshgrid(
        np.arange(cycles), np.arange(X), np.arange(K), np.arange(Z), indexing="ij"
    )
    return (((x * Z + z) * K + k) * cycles + c).reshape(-1)


def block_kernel(
    dims,
    grid_in,
    table_in,
    inverse_in,
    perm_in,
    basis_in,
    mix_in,
    gain_in,
    quad_in,
    conv_in,
    lat_off,
    lon_off,
    norm_in,
    up_in,
    down_in,
    out,
    grid_v,
    table,
    inverse,
    perm,
    basis,
    mix_all,
    up_w,
    down_w,
    leg,
    leg_t,
    z1_send,
    z1_recv,
    x1_send,
    x1_recv,
    acc,
    scaled,
    x2_send,
    x2_recv,
    z2_send,
    z2_recv,
    halo,
    padded,
    local_send,
    local_recv,
    field_send,
    field_recv,
    out_send,
    out_recv,
    load_sem,
    send_sem,
    recv_sem,
):
    X, Z, K, Y, cycles, modes, L, nlon, width, step, size = dims
    Q = X * K
    R = Q * Z
    rows = 2 * Q * modes
    half = Q * modes
    x = lax.axis_index("lat_0")
    z = lax.axis_index("lat_1")
    k = lax.axis_index("lat_2")
    y = lax.axis_index("chan")
    q = x * K + k
    rank = (x * Z + z) * K + k

    loads = [
        (table_in, table),
        (grid_in, grid_v),
        (basis_in, basis),
        (perm_in, perm),
        (inverse_in, inverse),
        (up_in, up_w),
        (down_in, down_w),
        (mix_in, mix_all.at[y]),
    ]
    copies = [
        pltpu.make_async_copy(src, dst, load_sem.at[i]) for i, (src, dst) in enumerate(loads)
    ]
    for copy in copies:
        copy.start()

    def z_device(i):
        return {"lat_1": lax.rem(z + i, Z)}

    def q_device(i):
        other = lax.rem(q + i, Q)
        return {"lat_0": other // K, "lat_2": lax.rem(other, K)}

    def y_device(i):
        return {"chan": lax.rem(y + i, Y)}

    def rank_device(r):
        return {"lat_0": r // (Z * K), "lat_1": lax.rem(r // K, Z), "lat_2": lax.rem(r, K)}

    barrier = pltpu.get_barrier_semaphore()

    def greet(device):
        pl.semaphore_signal(barrier, inc=1, device_id=device, device_id_type=MESH_ID)

    @pl.loop(1, Z)
    def _(i):
        greet(z_device(i))

    @pl.loop(1, Q)
    def _(i):
        greet(q_device(i))

    @pl.loop(1, Y)
    def _(i):
        greet(y_device(i))

    @pl.when(rank > 0)
    def _():
        greet(rank_device(rank - 1))

    @pl.when(rank < R - 1)
    def _():
        greet(rank_device(rank + 1))

    def send(src, dst, at, device):
        pltpu.make_async_remote_copy(
            src_ref=src,
            dst_ref=dst,
            send_sem=send_sem.at[at],
            recv_sem=recv_sem.at[at],
            device_id=device,
            device_id_type=MESH_ID,
        ).start()

    def await_recv(ref, at):
        pltpu.make_async_copy(ref, ref, recv_sem.at[at]).wait()

    def await_send(ref, at):
        pltpu.make_async_copy(ref, ref, send_sem.at[at]).wait()

    Z1, X1, X2, Z2, FIELD, OUT = (n * cycles for n in range(6))
    LOCAL = 6 * cycles
    MIX = LOCAL + 1
    BEFORE = LOCAL + 2
    AFTER = LOCAL + 3
    EXTRA = LOCAL + 4

    def forward(c):
        spec = jnp.dot(table[...], grid_v[c], preferred_element_type=F32) * (1.0 / nlon)
        spec = spec.astype(BF16).reshape(Z, rows, width)
        z1_send[c] = spec

    def send_z(buf, land, c, at):
        @pl.loop(0, Z - 1)
        def _(i):
            far = Z - 1 - i
            offset = jnp.where(lax.rem(far, 2) == 1, (far + 1) // 2, Z - far // 2)
            other = lax.rem(z + offset, Z)
            send(buf.at[c, other], land.at[c, z], at + c, {"lat_1": other})

        land[c, z] = buf[c, z]

    def send_q(buf, land, c, at):
        @pl.loop(1, Q)
        def _(i):
            other = lax.rem(q + i, Q)
            device = {"lat_0": other // K, "lat_2": lax.rem(other, K)}
            send(buf.at[c, other], land.at[c, q], at + c, device)

        land[c, q] = buf[c, q]

    copies[0].wait()
    copies[1].wait()
    forward(0)
    greeted = (Z - 1) + (Q - 1) + (Y - 1)
    greeted = greeted + jnp.where(rank > 0, 1, 0) + jnp.where(rank < R - 1, 1, 0)
    pl.semaphore_wait(barrier, greeted)
    send_z(z1_send, z1_recv, 0, Z1)
    for c in range(1, cycles):
        forward(c)
        send_z(z1_send, z1_recv, c, Z1)

    @pl.when(rank < R - 1)
    def _():
        send(grid_v.at[cycles - 1], halo.at[0], BEFORE, rank_device(rank + 1))

    @pl.when(rank > 0)
    def _():
        send(grid_v.at[0], halo.at[1], AFTER, rank_device(rank - 1))

    copies[7].wait()

    @pl.loop(1, Y)
    def _(i):
        send(mix_all.at[y], mix_all.at[y], MIX, y_device(i))

    copies[2].wait()
    copies[3].wait()
    for j in range(modes):
        weighted = (basis[j] * quad_in[...]).astype(BF16)
        leg[j] = lax.dot_general(
            weighted, perm[...], (((1,), (1,)), ((), ())), preferred_element_type=F32
        ).astype(BF16)
        leg_t[j] = lax.dot_general(
            perm[...], basis[j].astype(BF16), (((1,), (1,)), ((), ())), preferred_element_type=F32
        ).astype(BF16)

    def to_wavenumbers(c):
        await_recv(z1_recv.at[c, pl.ds(0, Z - 1)], Z1 + c)
        turned = jnp.swapaxes(z1_recv[c].astype(F32), 0, 1).astype(BF16)
        turned = turned.reshape(2, Q, modes, Z, width)
        for j in range(modes):
            for part in range(2):
                x1_send[c, :, 2 * j + part] = turned[part, :, j]
        send_q(x1_send, x1_recv, c, X1)

    def legendre(c):
        await_recv(x1_recv.at[c, pl.ds(0, Q - 1)], X1 + c)
        for j in range(modes):
            parts = [x1_recv[c, :, 2 * j + part].reshape(Q * Z, width) for part in range(2)]
            values = jnp.concatenate(parts, axis=1)
            found = jnp.dot(
                leg[j, :, c * Q * Z : (c + 1) * Q * Z], values, preferred_element_type=F32
            )
            if c == 0:
                acc[j] = found
            else:
                acc[j] += found

    def local_field():
        pad = (padded.shape[1] - nlon) // 2

        def place(at, values):
            padded[at, pad : pad + nlon] = values
            padded[at, 0:pad] = values[nlon - pad :]
            padded[at, pad + nlon :] = values[:pad]

        for c in range(cycles):
            place(c + 1, grid_v[c].astype(F32))

        @pl.when(rank > 0)
        def _():
            await_recv(halo.at[0], BEFORE)
            place(0, halo[0].astype(F32))

        @pl.when(rank == 0)
        def _():
            padded[0] = jnp.zeros(padded.shape[1:], F32)

        @pl.when(rank < R - 1)
        def _():
            await_recv(halo.at[1], AFTER)
            place(cycles + 1, halo[1].astype(F32))

        @pl.when(rank == R - 1)
        def _():
            padded[cycles + 1] = jnp.zeros(padded.shape[1:], F32)

        taps = conv_in.shape[0]
        block = 5 * TILE if nlon % (5 * TILE) == 0 else TILE

        def sine(cycle):
            angle = jnp.full((1, width), cycle, jnp.int32).astype(F32)
            return jnp.sin(math.pi * (angle + 0.5) / (R * cycles))

        for c in range(cycles):
            own = rank * cycles + c
            here = sine(own)
            weights = [
                conv_in[tap : tap + 1, :] * (sine(own + lat_off[tap]) / here)
                for tap in range(taps)
            ]

            @pl.loop(0, nlon // block)
            def _(b):
                base = pl.multiple_of(b * block, TILE)
                total = padded[c + 1, pl.ds(pad + base, block), :]
                for tap in range(taps):
                    source = padded[
                        c + 1 + lat_off[tap], pl.ds(pad + base + lon_off[tap], block), :
                    ]
                    total = total + weights[tap] * source
                local_send[c, pl.ds(base, block), :] = total.astype(BF16)

        @pl.loop(1, Y)
        def _(i):
            other = lax.rem(y + i, Y)
            first = pl.multiple_of(other * step, TILE)
            send(
                local_send.at[:, pl.ds(first, size)],
                local_recv.at[y],
                LOCAL,
                {"chan": other},
            )

        mine = pl.multiple_of(y * step, TILE)
        local_recv[y] = local_send[:, pl.ds(mine, size)]

    to_wavenumbers(0)
    local_field()
    for c in range(1, cycles):
        to_wavenumbers(c)
        legendre(c - 1)
    legendre(cycles - 1)

    gain = jnp.transpose(jnp.broadcast_to(gain_in[...], (width, L)))
    gain = jnp.concatenate([gain, gain], axis=1)
    for j in range(modes):
        weight = jnp.where(rank * modes + j == 0, 1.0, 2.0).astype(F32)
        scaled[j] = (acc[j] * gain * weight).astype(BF16)
    for c in range(cycles):
        for j in range(modes):
            back = jnp.dot(
                leg_t[j, c * Q * Z : (c + 1) * Q * Z, :], scaled[j], preferred_element_type=F32
            ).astype(BF16)
            for part in range(2):
                piece = back[:, part * width : (part + 1) * width]
                x2_send[c, :, 2 * j + part] = piece.reshape(Q, Z, width)
        send_q(x2_send, x2_recv, c, X2)

    for c in range(cycles):
        await_recv(x2_recv.at[c, pl.ds(0, Q - 1)], X2 + c)
        parts = [
            x2_recv[c, a, 2 * j + part].astype(F32)
            for part in range(2)
            for a in range(Q)
            for j in range(modes)
        ]
        z2_send[c] = jnp.swapaxes(jnp.stack(parts), 0, 1).astype(BF16)
        send_z(z2_send, z2_recv, c, Z2)

    copies[4].wait()
    copies[5].wait()
    copies[6].wait()
    await_recv(mix_all.at[pl.ds(0, Y - 1)], MIX)
    await_recv(local_recv.at[pl.ds(0, Y - 1)], LOCAL)

    def to_points(c):
        await_recv(z2_recv.at[c, pl.ds(0, Z - 1)], Z2 + c)
        value = z2_recv[c]
        wide = value.astype(F32)
        turned = jnp.concatenate([-wide[:, half:], wide[:, :half]], axis=1).astype(BF16)
        both = jnp.concatenate(
            [value.reshape(Z * rows, width), turned.reshape(Z * rows, width)], axis=1
        )
        fields = jnp.dot(inverse[...], both, preferred_element_type=F32).astype(BF16)
        field_send[c, 0] = fields[:, :width]
        field_send[c, 1] = fields[:, width:]

        @pl.loop(1, Y)
        def _(i):
            other = lax.rem(y + i, Y)
            first = pl.multiple_of(other * step, TILE)
            send(
                field_send.at[c, :, pl.ds(first, size)],
                field_recv.at[c, y],
                FIELD + c,
                {"chan": other},
            )

        mine = pl.multiple_of(y * step, TILE)
        field_recv[c, y] = field_send[c, :, pl.ds(mine, size)]

    def perceptron(c):
        await_recv(field_recv.at[c, pl.ds(0, Y - 1)], FIELD + c)
        points = jnp.concatenate(
            [field_recv[c, a, part] for part in range(2) for a in range(Y)], axis=1
        )
        pieces = []
        for a in range(Y):
            weights = jnp.concatenate([mix_all[a, 0], mix_all[a, 1]], axis=0)
            pieces.append(jnp.dot(points, weights, preferred_element_type=F32))
        spectral = jnp.concatenate(pieces, axis=1)
        near = jnp.concatenate([local_recv[a, c] for a in range(Y)], axis=1)
        row = (spectral + near.astype(F32)).astype(BF16).astype(F32)
        center = jnp.mean(row, axis=-1, keepdims=True)
        off = row - center
        spread = jnp.mean(off * off, axis=-1, keepdims=True)
        normed = (off / jnp.sqrt(spread + 1e-05) * norm_in[...]).astype(BF16)
        hidden = jax.nn.gelu(
            jnp.dot(normed, up_w[...], preferred_element_type=F32), approximate=True
        ).astype(BF16)
        result = (jnp.dot(hidden, down_w[...], preferred_element_type=F32) + row).astype(BF16)
        for a in range(Y):
            out_send[c, a] = result[:, a * width : (a + 1) * width]
        mine = pl.multiple_of(y * step, TILE)

        @pl.loop(1, Y)
        def _(i):
            other = lax.rem(y + i, Y)
            send(
                out_send.at[c, other, pl.ds(0, step)],
                out_recv.at[c, pl.ds(mine, step)],
                OUT + c,
                {"chan": other},
            )

            @pl.when(y == Y - 1)
            def _():
                send(
                    out_send.at[c, other, pl.ds(step, size - step)],
                    out_recv.at[c, pl.ds(Y * step, size - step)],
                    EXTRA + c,
                    {"chan": other},
                )

        out_recv[c, pl.ds(mine, step), :] = out_send[c, y, 0:step]

        @pl.when(y == Y - 1)
        def _():
            out_recv[c, Y * step :, :] = out_send[c, y, step:]

    def finish(c):
        await_recv(out_recv.at[c, pl.ds(0, (Y - 1) * step)], OUT + c)

        @pl.when(y < Y - 1)
        def _():
            await_recv(out_recv.at[c, pl.ds(0, size - step)], EXTRA + c)

        pltpu.make_async_copy(out_recv.at[c], out.at[c], load_sem.at[len(loads) + c]).start()

    to_points(0)
    for c in range(1, cycles):
        to_points(c)
        perceptron(c - 1)
        if c > 1:
            finish(c - 2)
    perceptron(cycles - 1)
    finish(cycles - 2)
    finish(cycles - 1)

    for c in range(cycles):
        await_send(z1_send.at[c, pl.ds(0, Z - 1)], Z1 + c)
        await_send(z2_send.at[c, pl.ds(0, Z - 1)], Z2 + c)
        await_send(x1_send.at[c, pl.ds(0, Q - 1)], X1 + c)
        await_send(x2_send.at[c, pl.ds(0, Q - 1)], X2 + c)
        await_send(field_recv.at[c, pl.ds(0, Y - 1)], FIELD + c)
        await_send(out_recv.at[c, pl.ds(0, (Y - 1) * step)], OUT + c)

        @pl.when(y == Y - 1)
        def _():
            await_send(out_recv.at[c, pl.ds(0, (Y - 1) * (size - step))], EXTRA + c)

    await_send(local_recv.at[pl.ds(0, Y - 1)], LOCAL)
    await_send(mix_all.at[pl.ds(0, Y - 1)], MIX)

    @pl.when(rank < R - 1)
    def _():
        await_send(halo.at[0], BEFORE)

    @pl.when(rank > 0)
    def _():
        await_send(halo.at[1], AFTER)

    for c in range(cycles):
        pltpu.make_async_copy(out_recv.at[c], out.at[c], load_sem.at[len(loads) + c]).wait()


def on_device(
    sizes,
    grid,
    basis,
    mix_weight,
    spectral_gain,
    conv_weight,
    lat_offsets,
    lon_offsets,
    ln_gain,
    up_weight,
    down_weight,
):
    X, Z, K, Y = sizes
    cycles, nlon, width = grid.shape
    modes, L, nlat = basis.shape
    C = width * Y
    Q = X * K
    step = nlon // (Y * TILE) * TILE
    size = nlon - (Y - 1) * step
    rows = 2 * Q * modes
    table = transform_tables(X, Z, K, modes, nlon)
    inverse = np.ascontiguousarray(table.T)
    order = cycle_order(X, Z, K, cycles)
    perm = np.zeros((nlat, nlat), ml_dtypes.bfloat16)
    perm[np.arange(nlat), order] = 1
    theta = (math.pi * (np.arange(nlat, dtype=np.float32) + np.float32(0.5)) / nlat).astype(
        np.float32
    )
    quad = (np.float32(math.pi / nlat) * np.sin(theta)).astype(np.float32)[None, :]
    dims = (X, Z, K, Y, cycles, modes, L, nlon, width, step, size)
    any_space = pl.BlockSpec(memory_space=pl.ANY)
    vmem = pl.BlockSpec(memory_space=pltpu.VMEM)
    smem = pl.BlockSpec(memory_space=pltpu.SMEM)
    pad = 8
    n_sem = 7 * cycles + 4
    scratch = [
        pltpu.VMEM((cycles, nlon, width), BF16),
        pltpu.VMEM(table.shape, BF16),
        pltpu.VMEM(inverse.shape, BF16),
        pltpu.VMEM(perm.shape, BF16),
        pltpu.VMEM(basis.shape, F32),
        pltpu.VMEM((Y, 2, C, width), BF16),
        pltpu.VMEM(up_weight.shape, BF16),
        pltpu.VMEM(down_weight.shape, BF16),
        pltpu.VMEM((modes, L, nlat), BF16),
        pltpu.VMEM((modes, nlat, L), BF16),
        pltpu.VMEM((cycles, Z, rows, width), BF16),
        pltpu.VMEM((cycles, Z, rows, width), BF16),
        pltpu.VMEM((cycles, Q, 2 * modes, Z, width), BF16),
        pltpu.VMEM((cycles, Q, 2 * modes, Z, width), BF16),
        pltpu.VMEM((modes, L, 2 * width), F32),
        pltpu.VMEM((modes, L, 2 * width), BF16),
        pltpu.VMEM((cycles, Q, 2 * modes, Z, width), BF16),
        pltpu.VMEM((cycles, Q, 2 * modes, Z, width), BF16),
        pltpu.VMEM((cycles, Z, rows, width), BF16),
        pltpu.VMEM((cycles, Z, rows, width), BF16),
        pltpu.VMEM((2, nlon, width), BF16),
        pltpu.VMEM((cycles + 2, nlon + 2 * pad, width), F32),
        pltpu.VMEM((cycles, nlon, width), BF16),
        pltpu.VMEM((Y, cycles, size, width), BF16),
        pltpu.VMEM((cycles, 2, nlon, width), BF16),
        pltpu.VMEM((cycles, Y, 2, size, width), BF16),
        pltpu.VMEM((cycles, Y, size, width), BF16),
        pltpu.VMEM((cycles, nlon, width), BF16),
        pltpu.SemaphoreType.DMA((8 + cycles,)),
        pltpu.SemaphoreType.DMA((n_sem,)),
        pltpu.SemaphoreType.DMA((n_sem,)),
    ]
    return pl.pallas_call(
        functools.partial(block_kernel, dims),
        out_shape=jax.ShapeDtypeStruct(grid.shape, BF16),
        in_specs=[any_space] * 6
        + [vmem, vmem, vmem, smem, smem, vmem]
        + [any_space] * 2,
        out_specs=any_space,
        scratch_shapes=scratch,
        compiler_params=pltpu.CompilerParams(
            collective_id=0, has_side_effects=True, vmem_limit_bytes=56 * 1024 * 1024
        ),
        name="block",
    )(
        grid,
        jnp.asarray(table),
        jnp.asarray(inverse),
        jnp.asarray(perm),
        basis,
        mix_weight,
        spectral_gain.reshape(1, L),
        jnp.asarray(quad),
        conv_weight,
        lat_offsets,
        lon_offsets,
        ln_gain.reshape(1, C),
        up_weight,
        down_weight,
    )


def build(finer):
    sizes = tuple(finer.shape[a] for a in (*LAT, "chan"))
    return jax.shard_map(
        functools.partial(on_device, sizes),
        mesh=finer,
        in_specs=(
            P(LAT, None, "chan"),
            P(LAT, None, None),
            P(None, None, "chan"),
            P(),
            P(None, "chan"),
            P(),
            P(),
            P(),
            P(),
            P(),
        ),
        out_specs=P(LAT, None, "chan"),
        check_vma=False,
    )


def solution(mesh):
    return build(
        Mesh(mesh.devices.reshape(4, 16, 2, mesh.shape["chan"]), (*LAT, "chan"))
    )
```

time: 210 us -> 106 us (0.50)
  the two profiles are of different devices: /device:TPU:32 before, /device:TPU:4 now
where the time goes in v1:
time: 106 us; the launch traced here: 105 us
  Pallas kernels  102 us (96%)
  local copies, waits for them, and re-layouts  3.13 us (3%)
    pallas_call x1, Pallas kernels, on_device(): pl.pallas_call(functools.partial(block_kernel, dims), out_shape=jax.Shape...  102 us

profile of v1, /device:TPU:4, one launch (start us, length us, event | category | flops | bytes accessed | tf_op | source)
XLA Modules:
  0.0 105.3 jit_solution(7225794438289964877)
XLA Ops:
  0.0 1.2 %reshape.6.gain_in = f32[1,384]{1,0:T(1,128)} reshape(f32[384]{0:T(512)} %param.17) | data formatting | bytes 3072 | tf_op jit(solution)/shard_map/reshape | solution.py:578
  1.2 102.1 %block.1 = bf16[3,720,128]{2,1,0:T(8,128)(2,1)} custom-call(bf16[3,720,128]{2,1,0:T(8,128)(2,1)} %grid_in.1, bf16[768,720]{1,0:T(8,128)(2,1)} %constant.8.clone.table_in, bf16[720,768]{1,0:T(8,128)(2,1)} %constant.9.clone.inverse_in, bf16[384,384]{1,0:T(8,128)(2,1)} %constant.10.clone.perm_in, f32[3,384,384]{2,1,0:T(8,128)} %basis_in.1, ...), custom_call_target="tpu_custom_call" | custom-call | tf_op jit(solution)/shard_map/block/pallas_call | solution.py:559
  103.4 1.9 %copy.16 = bf16[3,720,128]{2,1,0:T(8,128)(2,1)} copy(bf16[3,720,128]{2,1,0:T(8,128)(2,1)} %block.1) | data formatting | bytes 1105920

commit v2 on v1

v2 whole, which is shorter than its diff:
```python
import functools
import math

import jax
import jax.numpy as jnp
import ml_dtypes
import numpy as np
from jax import lax
from jax.experimental import pallas as pl
from jax.experimental.pallas import tpu as pltpu
from jax.sharding import Mesh
from jax.sharding import PartitionSpec as P

LAT = ("lat_0", "lat_1", "lat_2")
MESH_ID = pl.DeviceIdType.MESH
TILE = 16
F32 = jnp.float32
BF16 = jnp.bfloat16


def transform_tables(X, Z, K, modes, nlon):
    j, z, ri, x, k = np.meshgrid(
        np.arange(modes), np.arange(Z), np.arange(2), np.arange(X), np.arange(K), indexing="ij"
    )
    m = (((x * Z + z) * K + k) * modes + j).reshape(modes, -1).astype(np.int64)
    part = ri.reshape(modes, -1)
    points = np.arange(nlon, dtype=np.int64)
    phase = (m[:, :, None] * points) % nlon
    angle = np.float32(2.0 * math.pi) * phase.astype(np.float32) / np.float32(nlon)
    table = np.where(part[:, :, None] == 0, np.cos(angle), -np.sin(angle)).astype(np.float32)
    return table.astype(ml_dtypes.bfloat16)


def cycle_order(X, Z, K, cycles):
    x, k, z, c = np.meshgrid(
        np.arange(X), np.arange(K), np.arange(Z), np.arange(cycles), indexing="ij"
    )
    return (((x * Z + z) * K + k) * cycles + c).reshape(-1)


def block_kernel(
    dims,
    grid_in,
    table_in,
    inverse_in,
    perm_in,
    basis_in,
    mix_in,
    gain_in,
    quad_in,
    conv_in,
    lat_off,
    lon_off,
    norm_in,
    up_in,
    down_in,
    out,
    grid_v,
    table,
    inverse,
    perm,
    basis,
    mix_v,
    mix_w,
    up_w,
    down_w,
    leg,
    leg_t,
    z1_send,
    z1_recv,
    x1_send,
    x1_recv,
    coeff,
    x2_send,
    x2_recv,
    z2_send,
    z2_recv,
    halo,
    padded,
    base,
    sum_send,
    sum_recv,
    out_send,
    out_recv,
    load_sem,
    send_sem,
    recv_sem,
):
    X, Z, K, Y, cycles, modes, L, nlon, width, step, size = dims
    Q = X * K
    R = Q * Z
    band = Z * cycles
    x = lax.axis_index("lat_0")
    z = lax.axis_index("lat_1")
    k = lax.axis_index("lat_2")
    y = lax.axis_index("chan")
    q = x * K + k
    rank = (x * Z + z) * K + k
    last = modes - 1
    pad = (padded.shape[1] - nlon) // 2

    loads = [(table_in.at[0], table.at[0]), (grid_in, grid_v)]
    loads += [(table_in.at[j], table.at[j]) for j in range(1, modes)]
    BASIS = len(loads)
    loads += [(basis_in, basis), (perm_in, perm), (mix_in, mix_v)]
    REST = len(loads)
    loads += [(inverse_in, inverse), (up_in, up_w), (down_in, down_w)]
    copies = [
        pltpu.make_async_copy(src, dst, load_sem.at[i]) for i, (src, dst) in enumerate(loads)
    ]
    def q_device(other):
        return {"lat_0": other // K, "lat_2": lax.rem(other, K)}

    def rank_device(r):
        return {"lat_0": r // (Z * K), "lat_1": lax.rem(r // K, Z), "lat_2": lax.rem(r, K)}

    barrier = pltpu.get_barrier_semaphore()

    def greet(device):
        pl.semaphore_signal(barrier, inc=1, device_id=device, device_id_type=MESH_ID)

    def ring_place(i):
        far = Z - 1 - i
        offset = jnp.where(lax.rem(far, 2) == 1, (far + 1) // 2, Z - far // 2)
        return lax.rem(z + offset, Z)

    @pl.loop(0, Z - 1)
    def _(i):
        greet({"lat_1": ring_place(i)})

    copies[0].start()
    copies[1].start()

    @pl.loop(1, Q)
    def _(i):
        greet(q_device(lax.rem(q + i, Q)))

    @pl.loop(1, Y)
    def _(i):
        greet({"chan": lax.rem(y + i, Y)})

    @pl.when(rank > 0)
    def _():
        greet(rank_device(rank - 1))

    @pl.when(rank < R - 1)
    def _():
        greet(rank_device(rank + 1))

    def send(src, dst, at, device):
        pltpu.make_async_remote_copy(
            src_ref=src,
            dst_ref=dst,
            send_sem=send_sem.at[at],
            recv_sem=recv_sem.at[at],
            device_id=device,
            device_id_type=MESH_ID,
        ).start()

    def await_recv(ref, at):
        pltpu.make_async_copy(ref, ref, recv_sem.at[at]).wait()

    def await_send(ref, at):
        pltpu.make_async_copy(ref, ref, send_sem.at[at]).wait()

    Z1, X1, X2, Z2, GATHER = (n * modes for n in range(5))
    LAST = 5 * modes
    SUM = LAST + cycles
    OUT = SUM + cycles
    EXTRA = OUT + cycles
    BEFORE = EXTRA + cycles
    AFTER = BEFORE + 1

    def forward(j):
        points = jnp.concatenate([grid_v[c] for c in range(cycles)], axis=1)
        spec = jnp.dot(table[j], points, preferred_element_type=F32) * (1.0 / nlon)
        spec = spec.astype(BF16)
        for c in range(cycles):
            z1_send[j, :, c] = spec[:, c * width : (c + 1) * width].reshape(Z, 2 * Q, width)

    def send_z(buf, land, j, at):
        @pl.loop(0, Z - 1)
        def _(i):
            other = ring_place(i)
            send(buf.at[j, other], land.at[j, z], at + j, {"lat_1": other})

        land[j, z] = buf[j, z]

    def send_q(buf, land, j, at):
        @pl.loop(1, Q)
        def _(i):
            other = lax.rem(q + i, Q)
            send(buf.at[j, other], land.at[j, q], at + j, q_device(other))

        land[j, q] = buf[j, q]

    copies[0].wait()
    copies[1].wait()
    for copy in copies[2:]:
        copy.start()
    forward(0)
    greeted = (Z - 1) + (Q - 1) + (Y - 1)
    greeted = greeted + jnp.where(rank > 0, 1, 0) + jnp.where(rank < R - 1, 1, 0)
    pl.semaphore_wait(barrier, greeted)
    send_z(z1_send, z1_recv, 0, Z1)

    for j in range(1, modes):
        copies[1 + j].wait()
        forward(j)
        send_z(z1_send, z1_recv, j, Z1)

    @pl.when(rank < R - 1)
    def _():
        send(grid_v.at[cycles - 1], halo.at[0], BEFORE, rank_device(rank + 1))

    @pl.when(rank > 0)
    def _():
        send(grid_v.at[0], halo.at[1], AFTER, rank_device(rank - 1))

    copies[BASIS].wait()
    copies[BASIS + 1].wait()
    for j in range(modes):
        weighted = (basis[j] * quad_in[...]).astype(BF16)
        leg[j] = lax.dot_general(
            weighted, perm[...], (((1,), (1,)), ((), ())), preferred_element_type=F32
        ).astype(BF16)
        leg_t[j] = lax.dot_general(
            perm[...], basis[j].astype(BF16), (((1,), (1,)), ((), ())), preferred_element_type=F32
        ).astype(BF16)
    copies[BASIS + 2].wait()
    for a in range(Y):
        real = mix_v[0, a * width : (a + 1) * width, :]
        imag = mix_v[1, a * width : (a + 1) * width, :]
        at = 2 * a * width
        mix_w[at : at + width, :width] = real
        mix_w[at : at + width, width:] = imag
        mix_w[at + width : at + 2 * width, :width] = -imag
        mix_w[at + width : at + 2 * width, width:] = real
    gain = jnp.transpose(jnp.broadcast_to(gain_in[...].reshape(1, L), (width, L)))

    def to_owners(j):
        await_recv(z1_recv.at[j, pl.ds(0, Z - 1)], Z1 + j)
        value = z1_recv[j].reshape(band, 2 * Q, width)
        turned = jnp.swapaxes(value.astype(F32), 0, 1).astype(BF16)
        for part in range(2):
            x1_send[j, :, part] = turned[part * Q : (part + 1) * Q]
        send_q(x1_send, x1_recv, j, X1)

    def legendre(j):
        await_recv(x1_recv.at[j, pl.ds(0, Q - 1)], X1 + j)
        parts = [x1_recv[j, :, part].reshape(Q * band, width) for part in range(2)]
        values = jnp.concatenate(parts, axis=1)
        coeff[j, y] = jnp.dot(leg[j], values, preferred_element_type=F32).astype(BF16)

        @pl.loop(1, Y)
        def _(i):
            send(coeff.at[j, y], coeff.at[j, y], GATHER + j, {"chan": lax.rem(y + i, Y)})

    def mix(j):
        await_recv(coeff.at[j, pl.ds(0, Y - 1)], GATHER + j)
        values = jnp.concatenate([coeff[j, a] for a in range(Y)], axis=1)
        mixed = jnp.dot(values, mix_w[...], preferred_element_type=F32)
        weight = jnp.where(rank * modes + j == 0, 1.0, 2.0).astype(F32)
        scale = gain * weight
        mixed = (mixed * jnp.concatenate([scale, scale], axis=1)).astype(BF16)
        back = jnp.dot(leg_t[j], mixed, preferred_element_type=F32).astype(BF16)
        for part in range(2):
            piece = back[:, part * width : (part + 1) * width]
            x2_send[j, :, part] = piece.reshape(Q, band, width)
        send_q(x2_send, x2_recv, j, X2)

    def to_cycles(j):
        await_recv(x2_recv.at[j, pl.ds(0, Q - 1)], X2 + j)
        parts = [x2_recv[j, a, part].astype(F32) for part in range(2) for a in range(Q)]
        turned = jnp.swapaxes(jnp.stack(parts), 0, 1).astype(BF16)
        z2_send[j] = turned.reshape(Z, cycles, 2 * Q, width)
        if j < last:
            send_z(z2_send, z2_recv, j, Z2)
        else:
            for c in range(cycles):

                @pl.loop(0, Z - 1)
                def _(i):
                    other = ring_place(i)
                    send(
                        z2_send.at[j, other, c],
                        z2_recv.at[j, z, c],
                        LAST + c,
                        {"lat_1": other},
                    )

            z2_recv[j, z] = z2_send[j, z]

    def place(at, values):
        padded[at, pad : pad + nlon] = values
        padded[at, 0:pad] = values[nlon - pad :]
        padded[at, pad + nlon :] = values[:pad]

    def pad_field():
        for c in range(cycles):
            place(c + 1, grid_v[c].astype(F32))

        @pl.when(rank > 0)
        def _():
            await_recv(halo.at[0], BEFORE)
            place(0, halo[0].astype(F32))

        @pl.when(rank == 0)
        def _():
            padded[0] = jnp.zeros(padded.shape[1:], F32)

        @pl.when(rank < R - 1)
        def _():
            await_recv(halo.at[1], AFTER)
            place(cycles + 1, halo[1].astype(F32))

        @pl.when(rank == R - 1)
        def _():
            padded[cycles + 1] = jnp.zeros(padded.shape[1:], F32)

    def sine(cycle):
        angle = jnp.full((1, width), cycle, jnp.int32).astype(F32)
        return jnp.sin(math.pi * (angle + 0.5) / (R * cycles))

    def local_field(c):
        taps = conv_in.shape[0]
        block = 5 * TILE if nlon % (5 * TILE) == 0 else TILE
        own = rank * cycles + c
        here = sine(own)
        weights = [
            conv_in[tap : tap + 1, :] * (sine(own + lat_off[tap]) / here) for tap in range(taps)
        ]

        @pl.loop(0, nlon // block)
        def _(b):
            first = pl.multiple_of(b * block, TILE)
            total = padded[c + 1, pl.ds(pad + first, block), :]
            for tap in range(taps):
                source = padded[c + 1 + lat_off[tap], pl.ds(pad + first + lon_off[tap], block), :]
                total = total + weights[tap] * source
            base[c, pl.ds(first, block), :] = total

    to_owners(0)
    legendre(0)
    for j in range(1, modes):
        to_owners(j)
        if j > 1:
            mix(j - 2)
        legendre(j)
        if j > 1:
            to_cycles(j - 2)
    for j in range(last - 1, modes):
        mix(j)
        to_cycles(j)
    pad_field()
    for c in range(cycles):
        local_field(c)
    for i in range(3):
        copies[REST + i].wait()

    def synthesize(j):
        await_recv(z2_recv.at[j, pl.ds(0, Z - 1)], Z2 + j)
        values = jnp.concatenate(
            [z2_recv[j, :, c].reshape(2 * R, width) for c in range(cycles)], axis=1
        )
        found = jnp.dot(inverse[j], values, preferred_element_type=F32)
        for c in range(cycles):
            base[c] += found[:, c * width : (c + 1) * width]

    mine = pl.multiple_of(y * step, TILE)

    def to_points(c):
        await_recv(z2_recv.at[last, pl.ds(0, Z - 1), c], LAST + c)
        value = z2_recv[last, :, c].reshape(2 * R, width)
        found = jnp.dot(inverse[last], value, preferred_element_type=F32)
        sum_send[c] = (base[c] + found).astype(BF16)

        @pl.loop(1, Y)
        def _(i):
            other = lax.rem(y + i, Y)
            first = pl.multiple_of(other * step, TILE)
            send(
                sum_send.at[c, pl.ds(first, size)], sum_recv.at[c, y], SUM + c, {"chan": other}
            )

        sum_recv[c, y] = sum_send[c, pl.ds(mine, size)]

    def perceptron(c):
        await_recv(sum_recv.at[c, pl.ds(0, Y - 1)], SUM + c)
        row = jnp.concatenate([sum_recv[c, a] for a in range(Y)], axis=1).astype(F32)
        center = jnp.mean(row, axis=-1, keepdims=True)
        off = row - center
        spread = jnp.mean(off * off, axis=-1, keepdims=True)
        normed = (off / jnp.sqrt(spread + 1e-05) * norm_in[...]).astype(BF16)
        hidden = jax.nn.gelu(
            jnp.dot(normed, up_w[...], preferred_element_type=F32), approximate=True
        ).astype(BF16)
        result = (jnp.dot(hidden, down_w[...], preferred_element_type=F32) + row).astype(BF16)
        for a in range(Y):
            out_send[c, a] = result[:, a * width : (a + 1) * width]

        @pl.loop(1, Y)
        def _(i):
            other = lax.rem(y + i, Y)
            send(
                out_send.at[c, other, pl.ds(0, step)],
                out_recv.at[c, pl.ds(mine, step)],
                OUT + c,
                {"chan": other},
            )

            @pl.when(y == Y - 1)
            def _():
                send(
                    out_send.at[c, other, pl.ds(step, size - step)],
                    out_recv.at[c, pl.ds(Y * step, size - step)],
                    EXTRA + c,
                    {"chan": other},
                )

        out_recv[c, pl.ds(mine, step), :] = out_send[c, y, 0:step]

        @pl.when(y == Y - 1)
        def _():
            out_recv[c, Y * step :, :] = out_send[c, y, step:]

    def finish(c):
        await_recv(out_recv.at[c, pl.ds(0, (Y - 1) * step)], OUT + c)

        @pl.when(y < Y - 1)
        def _():
            await_recv(out_recv.at[c, pl.ds(0, size - step)], EXTRA + c)

        pltpu.make_async_copy(out_recv.at[c], out.at[c], load_sem.at[len(loads) + c]).start()

    for j in range(last):
        synthesize(j)
    to_points(0)
    for c in range(1, cycles):
        to_points(c)
        perceptron(c - 1)
    perceptron(cycles - 1)
    for c in range(cycles):
        finish(c)

    for j in range(modes):
        await_send(z1_send.at[j, pl.ds(0, Z - 1)], Z1 + j)
        await_send(x1_send.at[j, pl.ds(0, Q - 1)], X1 + j)
        await_send(x2_send.at[j, pl.ds(0, Q - 1)], X2 + j)
        if j < last:
            await_send(z2_send.at[j, pl.ds(0, Z - 1)], Z2 + j)
        await_send(coeff.at[j, pl.ds(0, Y - 1)], GATHER + j)
    for c in range(cycles):
        await_send(z2_send.at[last, pl.ds(0, Z - 1), c], LAST + c)
        await_send(sum_recv.at[c, pl.ds(0, Y - 1)], SUM + c)
        await_send(out_recv.at[c, pl.ds(0, (Y - 1) * step)], OUT + c)

        @pl.when(y == Y - 1)
        def _():
            await_send(out_recv.at[c, pl.ds(0, (Y - 1) * (size - step))], EXTRA + c)

    @pl.when(rank < R - 1)
    def _():
        await_send(halo.at[0], BEFORE)

    @pl.when(rank > 0)
    def _():
        await_send(halo.at[1], AFTER)

    for c in range(cycles):
        pltpu.make_async_copy(out_recv.at[c], out.at[c], load_sem.at[len(loads) + c]).wait()


def on_device(
    sizes,
    grid,
    basis,
    mix_weight,
    spectral_gain,
    conv_weight,
    lat_offsets,
    lon_offsets,
    ln_gain,
    up_weight,
    down_weight,
):
    X, Z, K, Y = sizes
    cycles, nlon, width = grid.shape
    modes, L, nlat = basis.shape
    C = width * Y
    Q = X * K
    step = nlon // (Y * TILE) * TILE
    size = nlon - (Y - 1) * step
    table = transform_tables(X, Z, K, modes, nlon)
    inverse = np.ascontiguousarray(table.transpose(0, 2, 1))
    perm = np.zeros((nlat, nlat), ml_dtypes.bfloat16)
    perm[np.arange(nlat), cycle_order(X, Z, K, cycles)] = 1
    theta = (math.pi * (np.arange(nlat, dtype=np.float32) + np.float32(0.5)) / nlat).astype(
        np.float32
    )
    quad = (np.float32(math.pi / nlat) * np.sin(theta)).astype(np.float32)[None, :]
    dims = (X, Z, K, Y, cycles, modes, L, nlon, width, step, size)
    any_space = pl.BlockSpec(memory_space=pl.ANY)
    vmem = pl.BlockSpec(memory_space=pltpu.VMEM)
    smem = pl.BlockSpec(memory_space=pltpu.SMEM)
    pad = 8
    n_sem = 5 * modes + 4 * cycles + 2
    around_z = (modes, Z, cycles, 2 * Q, width)
    around_q = (modes, Q, 2, Z * cycles, width)
    scratch = [
        pltpu.VMEM((cycles, nlon, width), BF16),
        pltpu.VMEM(table.shape, BF16),
        pltpu.VMEM(inverse.shape, BF16),
        pltpu.VMEM(perm.shape, BF16),
        pltpu.VMEM(basis.shape, F32),
        pltpu.VMEM(mix_weight.shape, BF16),
        pltpu.VMEM((2 * C, 2 * width), BF16),
        pltpu.VMEM(up_weight.shape, BF16),
        pltpu.VMEM(down_weight.shape, BF16),
        pltpu.VMEM((modes, L, nlat), BF16),
        pltpu.VMEM((modes, nlat, L), BF16),
        pltpu.VMEM(around_z, BF16),
        pltpu.VMEM(around_z, BF16),
        pltpu.VMEM(around_q, BF16),
        pltpu.VMEM(around_q, BF16),
        pltpu.VMEM((modes, Y, L, 2 * width), BF16),
        pltpu.VMEM(around_q, BF16),
        pltpu.VMEM(around_q, BF16),
        pltpu.VMEM(around_z, BF16),
        pltpu.VMEM(around_z, BF16),
        pltpu.VMEM((2, nlon, width), BF16),
        pltpu.VMEM((cycles + 2, nlon + 2 * pad, width), F32),
        pltpu.VMEM((cycles, nlon, width), F32),
        pltpu.VMEM((cycles, nlon, width), BF16),
        pltpu.VMEM((cycles, Y, size, width), BF16),
        pltpu.VMEM((cycles, Y, size, width), BF16),
        pltpu.VMEM((cycles, nlon, width), BF16),
        pltpu.SemaphoreType.DMA((7 + modes + cycles,)),
        pltpu.SemaphoreType.DMA((n_sem,)),
        pltpu.SemaphoreType.DMA((n_sem,)),
    ]
    return pl.pallas_call(
        functools.partial(block_kernel, dims),
        out_shape=jax.ShapeDtypeStruct(grid.shape, BF16),
        in_specs=[any_space] * 6
        + [vmem, vmem, vmem, smem, smem, vmem]
        + [any_space] * 2,
        out_specs=any_space,
        scratch_shapes=scratch,
        compiler_params=pltpu.CompilerParams(
            collective_id=0, has_side_effects=True, vmem_limit_bytes=56 * 1024 * 1024
        ),
        name="block",
    )(
        grid,
        jnp.asarray(table),
        jnp.asarray(inverse),
        jnp.asarray(perm),
        basis,
        mix_weight,
        spectral_gain,
        jnp.asarray(quad),
        conv_weight,
        lat_offsets,
        lon_offsets,
        ln_gain.reshape(1, C),
        up_weight,
        down_weight,
    )


def build(finer):
    sizes = tuple(finer.shape[a] for a in (*LAT, "chan"))
    return jax.shard_map(
        functools.partial(on_device, sizes),
        mesh=finer,
        in_specs=(
            P(LAT, None, "chan"),
            P(LAT, None, None),
            P(None, None, "chan"),
            P(),
            P(None, "chan"),
            P(),
            P(),
            P(),
            P(),
            P(),
        ),
        out_specs=P(LAT, None, "chan"),
        check_vma=False,
    )


def solution(mesh):
    return build(
        Mesh(mesh.devices.reshape(4, 16, 2, mesh.shape["chan"]), (*LAT, "chan"))
    )
```

time: 106 us -> 96.4 us (0.909)
  the two profiles are of different devices: /device:TPU:4 before, /device:TPU:32 now
where the time goes in v2:
time: 96.4 us; the launch traced here: 96.2 us
  Pallas kernels  94.3 us (98%)
  local copies, waits for them, and re-layouts  1.89 us (2%)
    pallas_call x1, Pallas kernels, on_device(): pl.pallas_call(functools.partial(block_kernel, dims), out_shape=jax.Shape...  94.3 us

profile of v2, /device:TPU:32, one launch (start us, length us, event | category | flops | bytes accessed | tf_op | source)
XLA Modules:
  0.0 96.2 jit_solution(17368302991292539807)
XLA Ops:
  0.0 94.3 %block.1 = bf16[3,720,128]{2,1,0:T(8,128)(2,1)} custom-call(bf16[3,720,128]{2,1,0:T(8,128)(2,1)} %grid_in.1, bf16[3,256,720]{2,1,0:T(8,128)(2,1)} %constant.8.clone.table_in, bf16[3,720,256]{2,1,0:T(8,128)(2,1)} %constant.9.clone.inverse_in, bf16[384,384]{1,0:T(8,128)(2,1)} %constant.10.clone.perm_in, f32[3,384,384]{2,1,0:T(8,128)} %basis_in.1, ...), custom_call_target="tpu_custom_call" | custom-call | tf_op jit(solution)/shard_map/block/pallas_call | solution.py:542
  94.3 1.9 %copy.16 = bf16[3,720,128]{2,1,0:T(8,128)(2,1)} copy(bf16[3,720,128]{2,1,0:T(8,128)(2,1)} %block.1) | data formatting | bytes 1105920

commit v3 on v2

--- a/solution.py
+++ b/solution.py
@@ -32,8 +32,8 @@
 
 
 def cycle_order(X, Z, K, cycles):
-    x, k, z, c = np.meshgrid(
-        np.arange(X), np.arange(K), np.arange(Z), np.arange(cycles), indexing="ij"
+    c, x, k, z = np.meshgrid(
+        np.arange(cycles), np.arange(X), np.arange(K), np.arange(Z), indexing="ij"
     )
     return (((x * Z + z) * K + k) * cycles + c).reshape(-1)
 
@@ -60,7 +60,7 @@
     inverse,
     perm,
     basis,
-    mix_v,
+    mix_all,
     mix_w,
     up_w,
     down_w,
@@ -70,7 +70,7 @@
     z1_recv,
     x1_send,
     x1_recv,
-    coeff,
+    gathered,
     x2_send,
     x2_recv,
     z2_send,
@@ -78,10 +78,13 @@
     halo,
     padded,
     base,
+    local_send,
+    local_recv,
+    field_send,
+    field_recv,
     sum_send,
     sum_recv,
     out_send,
-    out_recv,
     load_sem,
     send_sem,
     recv_sem,
@@ -89,7 +92,6 @@
     X, Z, K, Y, cycles, modes, L, nlon, width, step, size = dims
     Q = X * K
     R = Q * Z
-    band = Z * cycles
     x = lax.axis_index("lat_0")
     z = lax.axis_index("lat_1")
     k = lax.axis_index("lat_2")
@@ -97,12 +99,15 @@
     q = x * K + k
     rank = (x * Z + z) * K + k
     last = modes - 1
+    early = pl.ds(0, last)
+    rest = pl.ds(1, cycles - 1)
+    plane = Q * Z
     pad = (padded.shape[1] - nlon) // 2
 
     loads = [(table_in.at[0], table.at[0]), (grid_in, grid_v)]
     loads += [(table_in.at[j], table.at[j]) for j in range(1, modes)]
     BASIS = len(loads)
-    loads += [(basis_in, basis), (perm_in, perm), (mix_in, mix_v)]
+    loads += [(basis_in, basis), (perm_in, perm), (mix_in, mix_all.at[y])]
     REST = len(loads)
     loads += [(inverse_in, inverse), (up_in, up_w), (down_in, down_w)]
     copies = [
@@ -163,13 +168,16 @@
     def await_send(ref, at):
         pltpu.make_async_copy(ref, ref, send_sem.at[at]).wait()
 
-    Z1, X1, X2, Z2, GATHER = (n * modes for n in range(5))
-    LAST = 5 * modes
-    SUM = LAST + cycles
-    OUT = SUM + cycles
+    Z1, X1, X2, X2_REST, GATHER = (n * modes for n in range(5))
+    EARLY = 5 * modes
+    LAST = EARLY + cycles
+    FIELD = LAST + cycles
+    OUT = FIELD + cycles
     EXTRA = OUT + cycles
-    BEFORE = EXTRA + cycles
-    AFTER = BEFORE + 1
+    LOCAL = EXTRA + cycles
+    MIX = LOCAL + 1
+    BEFORE = LOCAL + 2
+    AFTER = LOCAL + 3
 
     def forward(j):
         points = jnp.concatenate([grid_v[c] for c in range(cycles)], axis=1)
@@ -219,6 +227,12 @@
 
     copies[BASIS].wait()
     copies[BASIS + 1].wait()
+    copies[BASIS + 2].wait()
+
+    @pl.loop(1, Y)
+    def _(i):
+        send(mix_all.at[y], mix_all.at[y], MIX, {"chan": lax.rem(y + i, Y)})
+
     for j in range(modes):
         weighted = (basis[j] * quad_in[...]).astype(BF16)
         leg[j] = lax.dot_general(
@@ -227,10 +241,9 @@
         leg_t[j] = lax.dot_general(
             perm[...], basis[j].astype(BF16), (((1,), (1,)), ((), ())), preferred_element_type=F32
         ).astype(BF16)
-    copies[BASIS + 2].wait()
     for a in range(Y):
-        real = mix_v[0, a * width : (a + 1) * width, :]
-        imag = mix_v[1, a * width : (a + 1) * width, :]
+        real = mix_all[y, 0, a * width : (a + 1) * width, :]
+        imag = mix_all[y, 1, a * width : (a + 1) * width, :]
         at = 2 * a * width
         mix_w[at : at + width, :width] = real
         mix_w[at : at + width, width:] = imag
@@ -240,56 +253,74 @@
 
     def to_owners(j):
         await_recv(z1_recv.at[j, pl.ds(0, Z - 1)], Z1 + j)
-        value = z1_recv[j].reshape(band, 2 * Q, width)
-        turned = jnp.swapaxes(value.astype(F32), 0, 1).astype(BF16)
-        for part in range(2):
-            x1_send[j, :, part] = turned[part * Q : (part + 1) * Q]
+        for c in range(cycles):
+            turned = jnp.swapaxes(z1_recv[j, :, c].astype(F32), 0, 1).astype(BF16)
+            for part in range(2):
+                x1_send[j, :, part, c] = turned[part * Q : (part + 1) * Q]
         send_q(x1_send, x1_recv, j, X1)
+
+    def send_rows(j, cut, at):
+        @pl.loop(1, Q)
+        def _(i):
+            other = lax.rem(q + i, Q)
+            send(x2_send.at[j, other, cut], x2_recv.at[j, q, cut], at + j, q_device(other))
 
     def legendre(j):
         await_recv(x1_recv.at[j, pl.ds(0, Q - 1)], X1 + j)
-        parts = [x1_recv[j, :, part].reshape(Q * band, width) for part in range(2)]
+        parts = [
+            jnp.concatenate(
+                [x1_recv[j, :, part, c].reshape(plane, width) for c in range(cycles)], axis=0
+            )
+            for part in range(2)
+        ]
         values = jnp.concatenate(parts, axis=1)
-        coeff[j, y] = jnp.dot(leg[j], values, preferred_element_type=F32).astype(BF16)
+        found = jnp.dot(leg[j], values, preferred_element_type=F32)
+        weight = jnp.where(rank * modes + j == 0, 1.0, 2.0).astype(F32)
+        scale = gain * weight
+        scaled = (found * jnp.concatenate([scale, scale], axis=1)).astype(BF16)
+        back = jnp.dot(leg_t[j], scaled, preferred_element_type=F32).astype(BF16)
+        for part in range(2):
+            piece = back[:plane, part * width : (part + 1) * width]
+            x2_send[j, :, 0, part] = piece.reshape(Q, Z, width)
+        send_rows(j, pl.ds(0, 1), X2)
+        x2_recv[j, q, 0] = x2_send[j, q, 0]
+        gathered[j, y] = back[plane:]
 
         @pl.loop(1, Y)
         def _(i):
-            send(coeff.at[j, y], coeff.at[j, y], GATHER + j, {"chan": lax.rem(y + i, Y)})
+            send(gathered.at[j, y], gathered.at[j, y], GATHER + j, {"chan": lax.rem(y + i, Y)})
 
     def mix(j):
-        await_recv(coeff.at[j, pl.ds(0, Y - 1)], GATHER + j)
-        values = jnp.concatenate([coeff[j, a] for a in range(Y)], axis=1)
-        mixed = jnp.dot(values, mix_w[...], preferred_element_type=F32)
-        weight = jnp.where(rank * modes + j == 0, 1.0, 2.0).astype(F32)
-        scale = gain * weight
-        mixed = (mixed * jnp.concatenate([scale, scale], axis=1)).astype(BF16)
-        back = jnp.dot(leg_t[j], mixed, preferred_element_type=F32).astype(BF16)
-        for part in range(2):
-            piece = back[:, part * width : (part + 1) * width]
-            x2_send[j, :, part] = piece.reshape(Q, band, width)
-        send_q(x2_send, x2_recv, j, X2)
-
-    def to_cycles(j):
-        await_recv(x2_recv.at[j, pl.ds(0, Q - 1)], X2 + j)
-        parts = [x2_recv[j, a, part].astype(F32) for part in range(2) for a in range(Q)]
-        turned = jnp.swapaxes(jnp.stack(parts), 0, 1).astype(BF16)
-        z2_send[j] = turned.reshape(Z, cycles, 2 * Q, width)
-        if j < last:
-            send_z(z2_send, z2_recv, j, Z2)
+        await_recv(gathered.at[j, pl.ds(0, Y - 1)], GATHER + j)
+        values = jnp.concatenate([gathered[j, a] for a in range(Y)], axis=1)
+        mixed = jnp.dot(values, mix_w[...], preferred_element_type=F32).astype(BF16)
+        for c in range(1, cycles):
+            for part in range(2):
+                piece = mixed[(c - 1) * plane : c * plane, part * width : (part + 1) * width]
+                x2_send[j, :, c, part] = piece.reshape(Q, Z, width)
+        send_rows(j, rest, X2_REST)
+        x2_recv[j, q, 1:] = x2_send[j, q, 1:]
+
+    def to_cycles(j, which):
+        if which == [0]:
+            await_recv(x2_recv.at[j, pl.ds(0, Q - 1), 0], X2 + j)
         else:
-            for c in range(cycles):
-
-                @pl.loop(0, Z - 1)
-                def _(i):
-                    other = ring_place(i)
-                    send(
-                        z2_send.at[j, other, c],
-                        z2_recv.at[j, z, c],
-                        LAST + c,
-                        {"lat_1": other},
-                    )
-
-            z2_recv[j, z] = z2_send[j, z]
+            await_recv(x2_recv.at[j, pl.ds(0, Q - 1), rest], X2_REST + j)
+        for c in which:
+            parts = [x2_recv[j, a, c, part].astype(F32) for part in range(2) for a in range(Q)]
+            z2_send[j, :, c] = jnp.swapaxes(jnp.stack(parts), 0, 1).astype(BF16)
+
+            @pl.loop(0, Z - 1)
+            def _(i):
+                other = ring_place(i)
+                send(
+                    z2_send.at[j, other, c],
+                    z2_recv.at[j, z, c],
+                    (LAST if j == last else EARLY) + c,
+                    {"lat_1": other},
+                )
+
+            z2_recv[j, z, c] = z2_send[j, z, c]
 
     def place(at, values):
         padded[at, pad : pad + nlon] = values
@@ -338,56 +369,95 @@
             for tap in range(taps):
                 source = padded[c + 1 + lat_off[tap], pl.ds(pad + first + lon_off[tap], block), :]
                 total = total + weights[tap] * source
-            base[c, pl.ds(first, block), :] = total
-
+            if c == 0:
+                local_send[pl.ds(first, block), :] = total.astype(BF16)
+            else:
+                base[c - 1, pl.ds(first, block), :] = total
+
+    mine = pl.multiple_of(y * step, TILE)
+
+    def share(src, dst, at):
+        @pl.loop(1, Y)
+        def _(i):
+            other = lax.rem(y + i, Y)
+            first = pl.multiple_of(other * step, TILE)
+            part = (slice(None),) * (len(src.shape) - 2) + (pl.ds(first, size),)
+            send(src.at[part], dst.at[y], at, {"chan": other})
+
+    def share_local():
+        pad_field()
+        for c in range(cycles):
+            local_field(c)
+        share(local_send, local_recv, LOCAL)
+        local_recv[y] = local_send[pl.ds(mine, size)]
+
+    later = list(range(1, cycles))
     to_owners(0)
     legendre(0)
     for j in range(1, modes):
         to_owners(j)
+        to_cycles(j - 1, [0])
         if j > 1:
-            mix(j - 2)
+            to_cycles(j - 2, later)
         legendre(j)
-        if j > 1:
-            to_cycles(j - 2)
-    for j in range(last - 1, modes):
-        mix(j)
-        to_cycles(j)
-    pad_field()
-    for c in range(cycles):
-        local_field(c)
+        mix(j - 1)
+    share_local()
+    to_cycles(last, [0])
+    if last > 0:
+        to_cycles(last - 1, later)
+    mix(last)
     for i in range(3):
         copies[REST + i].wait()
-
-    def synthesize(j):
-        await_recv(z2_recv.at[j, pl.ds(0, Z - 1)], Z2 + j)
-        values = jnp.concatenate(
-            [z2_recv[j, :, c].reshape(2 * R, width) for c in range(cycles)], axis=1
-        )
-        found = jnp.dot(inverse[j], values, preferred_element_type=F32)
-        for c in range(cycles):
-            base[c] += found[:, c * width : (c + 1) * width]
-
-    mine = pl.multiple_of(y * step, TILE)
+    to_cycles(last, later)
+    await_recv(mix_all.at[pl.ds(0, Y - 1)], MIX)
+    await_recv(local_recv.at[pl.ds(0, Y - 1)], LOCAL)
+
+    def both_parts(value):
+        wide = value.astype(F32)
+        turned = jnp.concatenate([-wide[:, Q:], wide[:, :Q]], axis=1).astype(BF16)
+        return [value.reshape(2 * R, width), turned.reshape(2 * R, width)]
 
     def to_points(c):
-        await_recv(z2_recv.at[last, pl.ds(0, Z - 1), c], LAST + c)
-        value = z2_recv[last, :, c].reshape(2 * R, width)
-        found = jnp.dot(inverse[last], value, preferred_element_type=F32)
-        sum_send[c] = (base[c] + found).astype(BF16)
-
-        @pl.loop(1, Y)
-        def _(i):
-            other = lax.rem(y + i, Y)
-            first = pl.multiple_of(other * step, TILE)
-            send(
-                sum_send.at[c, pl.ds(first, size)], sum_recv.at[c, y], SUM + c, {"chan": other}
+        def values(j):
+            value = z2_recv[j, :, c]
+            if c == 0:
+                return jnp.concatenate(both_parts(value), axis=1)
+            return value.reshape(2 * R, width)
+
+        await_recv(z2_recv.at[early, pl.ds(0, Z - 1), c], EARLY + c)
+        found = base[c - 1] if c > 0 else None
+        for j in range(modes):
+            if j == last:
+                await_recv(z2_recv.at[last, pl.ds(0, Z - 1), c], LAST + c)
+            term = jnp.dot(inverse[j], values(j), preferred_element_type=F32)
+            found = term if found is None else found + term
+        if c == 0:
+            fields = found.astype(BF16)
+            field_send[0] = fields[:, :width]
+            field_send[1] = fields[:, width:]
+            share(field_send, field_recv, FIELD)
+            field_recv[y] = field_send[:, pl.ds(mine, size)]
+        else:
+            sum_send[c - 1] = found.astype(BF16)
+            share(sum_send.at[c - 1], sum_recv.at[c - 1], FIELD + c)
+            sum_recv[c - 1, y] = sum_send[c - 1, pl.ds(mine, size)]
+
+    def perceptron(c):
+        if c == 0:
+            await_recv(field_recv.at[pl.ds(0, Y - 1)], FIELD)
+            points = jnp.concatenate(
+                [field_recv[a, part] for part in range(2) for a in range(Y)], axis=1
             )
-
-        sum_recv[c, y] = sum_send[c, pl.ds(mine, size)]
-
-    def perceptron(c):
-        await_recv(sum_recv.at[c, pl.ds(0, Y - 1)], SUM + c)
-        row = jnp.concatenate([sum_recv[c, a] for a in range(Y)], axis=1).astype(F32)
+            pieces = []
+            for a in range(Y):
+                weights = jnp.concatenate([mix_all[a, 0], mix_all[a, 1]], axis=0)
+                pieces.append(jnp.dot(points, weights, preferred_element_type=F32))
+            near = jnp.concatenate([local_recv[a] for a in range(Y)], axis=1)
+            row = (jnp.concatenate(pieces, axis=1) + near.astype(F32)).astype(BF16)
+        else:
+            await_recv(sum_recv.at[c - 1, pl.ds(0, Y - 1)], FIELD + c)
+            row = jnp.concatenate([sum_recv[c - 1, a] for a in range(Y)], axis=1)
+        row = row.astype(F32)
         center = jnp.mean(row, axis=-1, keepdims=True)
         off = row - center
         spread = jnp.mean(off * off, axis=-1, keepdims=True)
@@ -404,7 +474,7 @@
             other = lax.rem(y + i, Y)
             send(
                 out_send.at[c, other, pl.ds(0, step)],
-                out_recv.at[c, pl.ds(mine, step)],
+                out.at[c, pl.ds(mine, step)],
                 OUT + c,
                 {"chan": other},
             )
@@ -413,28 +483,25 @@
             def _():
                 send(
                     out_send.at[c, other, pl.ds(step, size - step)],
-                    out_recv.at[c, pl.ds(Y * step, size - step)],
+                    out.at[c, pl.ds(Y * step, size - step)],
                     EXTRA + c,
                     {"chan": other},
                 )
 
-        out_recv[c, pl.ds(mine, step), :] = out_send[c, y, 0:step]
+        out[c, pl.ds(mine, step), :] = out_send[c, y, 0:step]
 
         @pl.when(y == Y - 1)
         def _():
-            out_recv[c, Y * step :, :] = out_send[c, y, step:]
+            out[c, Y * step :, :] = out_send[c, y, step:]
 
     def finish(c):
-        await_recv(out_recv.at[c, pl.ds(0, (Y - 1) * step)], OUT + c)
+        await_recv(out.at[c, pl.ds(0, (Y - 1) * step)], OUT + c)
 
         @pl.when(y < Y - 1)
         def _():
-            await_recv(out_recv.at[c, pl.ds(0, size - step)], EXTRA + c)
-
-        pltpu.make_async_copy(out_recv.at[c], out.at[c], load_sem.at[len(loads) + c]).start()
-
-    for j in range(last):
-        synthesize(j)
+            await_recv(out.at[c, pl.ds(0, size - step)], EXTRA + c)
+
+
     to_points(0)
     for c in range(1, cycles):
         to_points(c)
@@ -446,18 +513,23 @@
     for j in range(modes):
         await_send(z1_send.at[j, pl.ds(0, Z - 1)], Z1 + j)
         await_send(x1_send.at[j, pl.ds(0, Q - 1)], X1 + j)
-        await_send(x2_send.at[j, pl.ds(0, Q - 1)], X2 + j)
-        if j < last:
-            await_send(z2_send.at[j, pl.ds(0, Z - 1)], Z2 + j)
-        await_send(coeff.at[j, pl.ds(0, Y - 1)], GATHER + j)
+        await_send(x2_send.at[j, pl.ds(0, Q - 1), 0], X2 + j)
+        await_send(x2_send.at[j, pl.ds(0, Q - 1), rest], X2_REST + j)
+        await_send(gathered.at[j, pl.ds(0, Y - 1)], GATHER + j)
+    await_send(local_recv.at[pl.ds(0, Y - 1)], LOCAL)
+    await_send(mix_all.at[pl.ds(0, Y - 1)], MIX)
     for c in range(cycles):
+        await_send(z2_send.at[early, pl.ds(0, Z - 1), c], EARLY + c)
         await_send(z2_send.at[last, pl.ds(0, Z - 1), c], LAST + c)
-        await_send(sum_recv.at[c, pl.ds(0, Y - 1)], SUM + c)
-        await_send(out_recv.at[c, pl.ds(0, (Y - 1) * step)], OUT + c)
+        if c == 0:
+            await_send(field_recv.at[pl.ds(0, Y - 1)], FIELD)
+        else:
+            await_send(sum_recv.at[c - 1, pl.ds(0, Y - 1)], FIELD + c)
+        await_send(out.at[c, pl.ds(0, (Y - 1) * step)], OUT + c)
 
         @pl.when(y == Y - 1)
         def _():
-            await_send(out_recv.at[c, pl.ds(0, (Y - 1) * (size - step))], EXTRA + c)
+            await_send(out.at[c, pl.ds(0, (Y - 1) * (size - step))], EXTRA + c)
 
     @pl.when(rank < R - 1)
     def _():
@@ -466,9 +538,6 @@
     @pl.when(rank > 0)
     def _():
         await_send(halo.at[1], AFTER)
-
-    for c in range(cycles):
-        pltpu.make_async_copy(out_recv.at[c], out.at[c], load_sem.at[len(loads) + c]).wait()
 
 
 def on_device(
@@ -504,16 +573,17 @@
     vmem = pl.BlockSpec(memory_space=pltpu.VMEM)
     smem = pl.BlockSpec(memory_space=pltpu.SMEM)
     pad = 8
-    n_sem = 5 * modes + 4 * cycles + 2
+    n_sem = 5 * modes + 5 * cycles + 4
     around_z = (modes, Z, cycles, 2 * Q, width)
-    around_q = (modes, Q, 2, Z * cycles, width)
+    around_q = (modes, Q, 2, cycles, Z, width)
+    around_back = (modes, Q, cycles, 2, Z, width)
     scratch = [
         pltpu.VMEM((cycles, nlon, width), BF16),
         pltpu.VMEM(table.shape, BF16),
         pltpu.VMEM(inverse.shape, BF16),
         pltpu.VMEM(perm.shape, BF16),
         pltpu.VMEM(basis.shape, F32),
-        pltpu.VMEM(mix_weight.shape, BF16),
+        pltpu.VMEM((Y, 2, C, width), BF16),
         pltpu.VMEM((2 * C, 2 * width), BF16),
         pltpu.VMEM(up_weight.shape, BF16),
         pltpu.VMEM(down_weight.shape, BF16),
@@ -523,29 +593,32 @@
         pltpu.VMEM(around_z, BF16),
         pltpu.VMEM(around_q, BF16),
         pltpu.VMEM(around_q, BF16),
-        pltpu.VMEM((modes, Y, L, 2 * width), BF16),
-        pltpu.VMEM(around_q, BF16),
-        pltpu.VMEM(around_q, BF16),
+        pltpu.VMEM((modes, Y, (cycles - 1) * Q * Z, 2 * width), BF16),
+        pltpu.VMEM(around_back, BF16),
+        pltpu.VMEM(around_back, BF16),
         pltpu.VMEM(around_z, BF16),
         pltpu.VMEM(around_z, BF16),
         pltpu.VMEM((2, nlon, width), BF16),
         pltpu.VMEM((cycles + 2, nlon + 2 * pad, width), F32),
-        pltpu.VMEM((cycles, nlon, width), F32),
-        pltpu.VMEM((cycles, nlon, width), BF16),
+        pltpu.VMEM((cycles - 1, nlon, width), F32),
+        pltpu.VMEM((nlon, width), BF16),
+        pltpu.VMEM((Y, size, width), BF16),
+        pltpu.VMEM((2, nlon, width), BF16),
+        pltpu.VMEM((Y, 2, size, width), BF16),
+        pltpu.VMEM((cycles - 1, nlon, width), BF16),
+        pltpu.VMEM((cycles - 1, Y, size, width), BF16),
         pltpu.VMEM((cycles, Y, size, width), BF16),
-        pltpu.VMEM((cycles, Y, size, width), BF16),
-        pltpu.VMEM((cycles, nlon, width), BF16),
-        pltpu.SemaphoreType.DMA((7 + modes + cycles,)),
+        pltpu.SemaphoreType.DMA((7 + modes,)),
         pltpu.SemaphoreType.DMA((n_sem,)),
         pltpu.SemaphoreType.DMA((n_sem,)),
     ]
     return pl.pallas_call(
         functools.partial(block_kernel, dims),
-        out_shape=jax.ShapeDtypeStruct(grid.shape, BF16),
+        out_shape=pltpu.VMEM(grid.shape, BF16),
         in_specs=[any_space] * 6
         + [vmem, vmem, vmem, smem, smem, vmem]
         + [any_space] * 2,
-        out_specs=any_space,
+        out_specs=vmem,
         scratch_shapes=scratch,
         compiler_params=pltpu.CompilerParams(
             collective_id=0, has_side_effects=True, vmem_limit_bytes=56 * 1024 * 1024

time: 96.4 us -> 88.5 us (0.918)
  the two profiles are of different devices: /device:TPU:32 before, /device:TPU:4 now
where the time goes in v3:
time: 88.5 us; the launch traced here: 88.4 us
  Pallas kernels  87.5 us (99%)
    pallas_call x1, Pallas kernels, on_device(): pl.pallas_call(functools.partial(block_kernel, dims), out_shape=pltpu.VME...  87.5 us

profile of v3, /device:TPU:4, one launch (start us, length us, event | category | flops | bytes accessed | tf_op | source)
XLA Modules:
  0.0 88.4 jit_solution(13634843961345564522)
XLA Ops:
  0.0 87.5 %block.1 = bf16[3,720,128]{2,1,0:T(8,128)(2,1)S(1)} custom-call(bf16[3,720,128]{2,1,0:T(8,128)(2,1)} %grid_in.1, bf16[3,256,720]{2,1,0:T(8,128)(2,1)} %constant.8.clone.table_in, bf16[3,720,256]{2,1,0:T(8,128)(2,1)} %constant.9.clone.inverse_in, bf16[384,384]{1,0:T(8,128)(2,1)} %constant.10.clone.perm_in, f32[3,384,384]{2,1,0:T(8,128)} %basis_in.1, ...), custom_call_target="tpu_custom_call" | custom-call | tf_op jit(solution)/shard_map/block/pallas_call | solution.py:615
  87.6 0.8 copy.16

commit v4 on v3

--- a/solution.py
+++ b/solution.py
@@ -46,15 +46,21 @@
     perm_in,
     basis_in,
     mix_in,
+    gain_hbm,
+    quad_hbm,
+    conv_hbm,
+    lat_hbm,
+    lon_hbm,
+    norm_hbm,
+    up_in,
+    down_in,
+    out,
     gain_in,
     quad_in,
     conv_in,
     lat_off,
     lon_off,
     norm_in,
-    up_in,
-    down_in,
-    out,
     grid_v,
     table,
     inverse,
@@ -78,6 +84,7 @@
     halo,
     padded,
     base,
+    fields0,
     local_send,
     local_recv,
     field_send,
@@ -108,8 +115,10 @@
     loads += [(table_in.at[j], table.at[j]) for j in range(1, modes)]
     BASIS = len(loads)
     loads += [(basis_in, basis), (perm_in, perm), (mix_in, mix_all.at[y])]
+    loads += [(gain_hbm, gain_in), (quad_hbm, quad_in)]
     REST = len(loads)
     loads += [(inverse_in, inverse), (up_in, up_w), (down_in, down_w)]
+    loads += [(conv_hbm, conv_in), (lat_hbm, lat_off), (lon_hbm, lon_off), (norm_hbm, norm_in)]
     copies = [
         pltpu.make_async_copy(src, dst, load_sem.at[i]) for i, (src, dst) in enumerate(loads)
     ]
@@ -178,6 +187,9 @@
     MIX = LOCAL + 1
     BEFORE = LOCAL + 2
     AFTER = LOCAL + 3
+    FIELD_TAIL = LOCAL + 4
+    OUT_TAIL = LOCAL + 5
+    cut = size // 2 // TILE * TILE
 
     def forward(j):
         points = jnp.concatenate([grid_v[c] for c in range(cycles)], axis=1)
@@ -228,6 +240,8 @@
     copies[BASIS].wait()
     copies[BASIS + 1].wait()
     copies[BASIS + 2].wait()
+    copies[BASIS + 3].wait()
+    copies[BASIS + 4].wait()
 
     @pl.loop(1, Y)
     def _(i):
@@ -376,13 +390,20 @@
 
     mine = pl.multiple_of(y * step, TILE)
 
-    def share(src, dst, at):
+    def share(src, dst, at, low=0, rows=None):
+        rows = size if rows is None else rows
+
         @pl.loop(1, Y)
         def _(i):
             other = lax.rem(y + i, Y)
-            first = pl.multiple_of(other * step, TILE)
-            part = (slice(None),) * (len(src.shape) - 2) + (pl.ds(first, size),)
-            send(src.at[part], dst.at[y], at, {"chan": other})
+            first = pl.multiple_of(other * step, TILE) + low
+            lead = (slice(None),) * (len(src.shape) - 2)
+            send(
+                src.at[(*lead, pl.ds(first, rows))],
+                dst.at[(y, *lead, pl.ds(low, rows))],
+                at,
+                {"chan": other},
+            )
 
     def share_local():
         pad_field()
@@ -401,36 +422,38 @@
             to_cycles(j - 2, later)
         legendre(j)
         mix(j - 1)
+    for copy in copies[REST:]:
+        copy.wait()
     share_local()
     to_cycles(last, [0])
     if last > 0:
         to_cycles(last - 1, later)
-    mix(last)
-    for i in range(3):
-        copies[REST + i].wait()
-    to_cycles(last, later)
-    await_recv(mix_all.at[pl.ds(0, Y - 1)], MIX)
-    await_recv(local_recv.at[pl.ds(0, Y - 1)], LOCAL)
-
     def both_parts(value):
         wide = value.astype(F32)
         turned = jnp.concatenate([-wide[:, Q:], wide[:, :Q]], axis=1).astype(BF16)
         return [value.reshape(2 * R, width), turned.reshape(2 * R, width)]
 
-    def to_points(c):
-        def values(j):
-            value = z2_recv[j, :, c]
-            if c == 0:
-                return jnp.concatenate(both_parts(value), axis=1)
-            return value.reshape(2 * R, width)
-
+    def values_of(j, c):
+        value = z2_recv[j, :, c]
+        if c == 0:
+            return jnp.concatenate(both_parts(value), axis=1)
+        return value.reshape(2 * R, width)
+
+    def partly(c):
         await_recv(z2_recv.at[early, pl.ds(0, Z - 1), c], EARLY + c)
         found = base[c - 1] if c > 0 else None
-        for j in range(modes):
-            if j == last:
-                await_recv(z2_recv.at[last, pl.ds(0, Z - 1), c], LAST + c)
-            term = jnp.dot(inverse[j], values(j), preferred_element_type=F32)
+        for j in range(last):
+            term = jnp.dot(inverse[j], values_of(j, c), preferred_element_type=F32)
             found = term if found is None else found + term
+        if c == 0:
+            fields0[...] = found
+        else:
+            base[c - 1] = found
+
+    def to_points(c):
+        await_recv(z2_recv.at[last, pl.ds(0, Z - 1), c], LAST + c)
+        found = fields0[...] if c == 0 else base[c - 1]
+        found = found + jnp.dot(inverse[last], values_of(last, c), preferred_element_type=F32)
         if c == 0:
             fields = found.astype(BF16)
             field_send[0] = fields[:, :width]
@@ -439,10 +462,17 @@
             field_recv[y] = field_send[:, pl.ds(mine, size)]
         else:
             sum_send[c - 1] = found.astype(BF16)
-            share(sum_send.at[c - 1], sum_recv.at[c - 1], FIELD + c)
+            if c == cycles - 1:
+                share(sum_send.at[c - 1], sum_recv.at[c - 1], FIELD + c, 0, cut)
+                share(sum_send.at[c - 1], sum_recv.at[c - 1], FIELD_TAIL, cut, size - cut)
+            else:
+                share(sum_send.at[c - 1], sum_recv.at[c - 1], FIELD + c)
             sum_recv[c - 1, y] = sum_send[c - 1, pl.ds(mine, size)]
 
-    def perceptron(c):
+    def perceptron(c, low=0, rows=None):
+        rows = size if rows is None else rows
+        own = slice(low, low + rows)
+        out_at, field_at = (OUT + c, FIELD + c) if low == 0 else (OUT_TAIL, FIELD_TAIL)
         if c == 0:
             await_recv(field_recv.at[pl.ds(0, Y - 1)], FIELD)
             points = jnp.concatenate(
@@ -455,8 +485,8 @@
             near = jnp.concatenate([local_recv[a] for a in range(Y)], axis=1)
             row = (jnp.concatenate(pieces, axis=1) + near.astype(F32)).astype(BF16)
         else:
-            await_recv(sum_recv.at[c - 1, pl.ds(0, Y - 1)], FIELD + c)
-            row = jnp.concatenate([sum_recv[c - 1, a] for a in range(Y)], axis=1)
+            await_recv(sum_recv.at[c - 1, pl.ds(0, Y - 1), pl.ds(low, rows)], field_at)
+            row = jnp.concatenate([sum_recv[c - 1, a, own] for a in range(Y)], axis=1)
         row = row.astype(F32)
         center = jnp.mean(row, axis=-1, keepdims=True)
         off = row - center
@@ -467,46 +497,69 @@
         ).astype(BF16)
         result = (jnp.dot(hidden, down_w[...], preferred_element_type=F32) + row).astype(BF16)
         for a in range(Y):
-            out_send[c, a] = result[:, a * width : (a + 1) * width]
+            out_send[c, a, own] = result[:, a * width : (a + 1) * width]
+        main = min(low + rows, step) - low
+        extra = low + rows > step
 
         @pl.loop(1, Y)
         def _(i):
             other = lax.rem(y + i, Y)
             send(
-                out_send.at[c, other, pl.ds(0, step)],
-                out.at[c, pl.ds(mine, step)],
-                OUT + c,
+                out_send.at[c, other, pl.ds(low, main)],
+                out.at[c, pl.ds(mine + low, main)],
+                out_at,
                 {"chan": other},
             )
 
+            if extra:
+
+                @pl.when(y == Y - 1)
+                def _():
+                    send(
+                        out_send.at[c, other, pl.ds(step, size - step)],
+                        out.at[c, pl.ds(Y * step, size - step)],
+                        EXTRA + c,
+                        {"chan": other},
+                    )
+
+        out[c, pl.ds(mine + low, main), :] = out_send[c, y, low : low + main]
+
+        if extra:
+
             @pl.when(y == Y - 1)
             def _():
-                send(
-                    out_send.at[c, other, pl.ds(step, size - step)],
-                    out.at[c, pl.ds(Y * step, size - step)],
-                    EXTRA + c,
-                    {"chan": other},
-                )
-
-        out[c, pl.ds(mine, step), :] = out_send[c, y, 0:step]
-
-        @pl.when(y == Y - 1)
-        def _():
-            out[c, Y * step :, :] = out_send[c, y, step:]
+                out[c, Y * step :, :] = out_send[c, y, step:]
+
+    def out_pieces(c):
+        if c < cycles - 1:
+            return [(OUT + c, step)]
+        return [(OUT + c, cut), (OUT_TAIL, step - cut)]
 
     def finish(c):
-        await_recv(out.at[c, pl.ds(0, (Y - 1) * step)], OUT + c)
+        for at, main in out_pieces(c):
+            await_recv(out.at[c, pl.ds(0, (Y - 1) * main)], at)
 
         @pl.when(y < Y - 1)
         def _():
             await_recv(out.at[c, pl.ds(0, size - step)], EXTRA + c)
 
 
+    partly(0)
+    mix(last)
     to_points(0)
+    to_cycles(last, later)
+    partly(1)
+    await_recv(mix_all.at[pl.ds(0, Y - 1)], MIX)
+    await_recv(local_recv.at[pl.ds(0, Y - 1)], LOCAL)
+    perceptron(0)
     for c in range(1, cycles):
+        if c > 1:
+            partly(c)
         to_points(c)
-        perceptron(c - 1)
-    perceptron(cycles - 1)
+    for c in range(1, cycles - 1):
+        perceptron(c)
+    perceptron(cycles - 1, 0, cut)
+    perceptron(cycles - 1, cut, size - cut)
     for c in range(cycles):
         finish(c)
 
@@ -523,9 +576,13 @@
         await_send(z2_send.at[last, pl.ds(0, Z - 1), c], LAST + c)
         if c == 0:
             await_send(field_recv.at[pl.ds(0, Y - 1)], FIELD)
+        elif c < cycles - 1:
+            await_send(sum_recv.at[c - 1, pl.ds(0, Y - 1)], FIELD + c)
         else:
-            await_send(sum_recv.at[c - 1, pl.ds(0, Y - 1)], FIELD + c)
-        await_send(out.at[c, pl.ds(0, (Y - 1) * step)], OUT + c)
+            await_send(sum_recv.at[c - 1, pl.ds(0, Y - 1), pl.ds(0, cut)], FIELD + c)
+            await_send(sum_recv.at[c - 1, pl.ds(0, Y - 1), pl.ds(cut, size - cut)], FIELD_TAIL)
+        for at, main in out_pieces(c):
+            await_send(out.at[c, pl.ds(0, (Y - 1) * main)], at)
 
         @pl.when(y == Y - 1)
         def _():
@@ -571,13 +628,18 @@
     dims = (X, Z, K, Y, cycles, modes, L, nlon, width, step, size)
     any_space = pl.BlockSpec(memory_space=pl.ANY)
     vmem = pl.BlockSpec(memory_space=pltpu.VMEM)
-    smem = pl.BlockSpec(memory_space=pltpu.SMEM)
     pad = 8
-    n_sem = 5 * modes + 5 * cycles + 4
+    n_sem = 5 * modes + 5 * cycles + 6
     around_z = (modes, Z, cycles, 2 * Q, width)
     around_q = (modes, Q, 2, cycles, Z, width)
     around_back = (modes, Q, cycles, 2, Z, width)
     scratch = [
+        pltpu.VMEM((L,), F32),
+        pltpu.VMEM((1, nlat), F32),
+        pltpu.VMEM(conv_weight.shape, F32),
+        pltpu.SMEM(lat_offsets.shape, jnp.int32),
+        pltpu.SMEM(lon_offsets.shape, jnp.int32),
+        pltpu.VMEM((1, C), F32),
         pltpu.VMEM((cycles, nlon, width), BF16),
         pltpu.VMEM(table.shape, BF16),
         pltpu.VMEM(inverse.shape, BF16),
@@ -601,6 +663,7 @@
         pltpu.VMEM((2, nlon, width), BF16),
         pltpu.VMEM((cycles + 2, nlon + 2 * pad, width), F32),
         pltpu.VMEM((cycles - 1, nlon, width), F32),
+        pltpu.VMEM((nlon, 2 * width), F32),
         pltpu.VMEM((nlon, width), BF16),
         pltpu.VMEM((Y, size, width), BF16),
         pltpu.VMEM((2, nlon, width), BF16),
@@ -608,16 +671,14 @@
         pltpu.VMEM((cycles - 1, nlon, width), BF16),
         pltpu.VMEM((cycles - 1, Y, size, width), BF16),
         pltpu.VMEM((cycles, Y, size, width), BF16),
-        pltpu.SemaphoreType.DMA((7 + modes,)),
+        pltpu.SemaphoreType.DMA((13 + modes,)),
         pltpu.SemaphoreType.DMA((n_sem,)),
         pltpu.SemaphoreType.DMA((n_sem,)),
     ]
     return pl.pallas_call(
         functools.partial(block_kernel, dims),
         out_shape=pltpu.VMEM(grid.shape, BF16),
-        in_specs=[any_space] * 6
-        + [vmem, vmem, vmem, smem, smem, vmem]
-        + [any_space] * 2,
+        in_specs=[any_space] * 14,
         out_specs=vmem,
         scratch_shapes=scratch,
         compiler_params=pltpu.CompilerParams(

time: 88.5 us -> 85.3 us (0.964)
  the two profiles are of different devices: /device:TPU:4 before, /device:TPU:2 now
where the time goes in v4:
time: 85.3 us; the launch traced here: 85.1 us
  Pallas kernels  84.3 us (99%)
    pallas_call x1, Pallas kernels, on_device(): pl.pallas_call(functools.partial(block_kernel, dims), out_shape=pltpu.VME...  84.3 us

profile of v4, /device:TPU:2, one launch (start us, length us, event | category | flops | bytes accessed | tf_op | source)
XLA Modules:
  0.0 85.1 jit_solution(1990906818893654502)
XLA Ops:
  0.0 84.3 %block.1 = bf16[3,720,128]{2,1,0:T(8,128)(2,1)S(1)} custom-call(bf16[3,720,128]{2,1,0:T(8,128)(2,1)} %grid_in.1, bf16[3,256,720]{2,1,0:T(8,128)(2,1)} %constant.8.clone.table_in, bf16[3,720,256]{2,1,0:T(8,128)(2,1)} %constant.9.clone.inverse_in, bf16[384,384]{1,0:T(8,128)(2,1)} %constant.10.clone.perm_in, f32[3,384,384]{2,1,0:T(8,128)} %basis_in.1, ...), custom_call_target="tpu_custom_call" | custom-call | tf_op jit(solution)/shard_map/block/pallas_call | solution.py:678
  84.3 0.8 copy.16

commit v5 on v4

--- a/solution.py
+++ b/solution.py
@@ -76,9 +76,12 @@
     z1_recv,
     x1_send,
     x1_recv,
+    rows_send,
     gathered,
+    mixed_send,
     x2_send,
     x2_recv,
+    late_recv,
     z2_send,
     z2_recv,
     halo,
@@ -107,11 +110,21 @@
     rank = (x * Z + z) * K + k
     last = modes - 1
     early = pl.ds(0, last)
-    rest = pl.ds(1, cycles - 1)
     plane = Q * Z
+    has_own = k == lax.rem(y, K)
+    n_late = (cycles - 1) * Q
     pad = (padded.shape[1] - nlon) // 2
 
-    loads = [(table_in.at[0], table.at[0]), (grid_in, grid_v)]
+    loads = []
+    middle = nlon // 2 // TILE * TILE
+    for low, rows in ((0, middle), (middle, nlon - middle)):
+        piece = pl.ds(low, rows)
+        loads += [(grid_in.at[c, piece], grid_v.at[c, piece]) for c in range(cycles)]
+    quarter = 2 * R // 4
+    for i in range(4):
+        piece = pl.ds(i * quarter, quarter)
+        loads.append((table_in.at[0, piece], table.at[0, piece]))
+    FIRST = len(loads)
     loads += [(table_in.at[j], table.at[j]) for j in range(1, modes)]
     BASIS = len(loads)
     loads += [(basis_in, basis), (perm_in, perm), (mix_in, mix_all.at[y])]
@@ -138,20 +151,17 @@
         offset = jnp.where(lax.rem(far, 2) == 1, (far + 1) // 2, Z - far // 2)
         return lax.rem(z + offset, Z)
 
+    for copy in copies[:FIRST]:
+        copy.start()
+
     @pl.loop(0, Z - 1)
     def _(i):
         greet({"lat_1": ring_place(i)})
 
-    copies[0].start()
-    copies[1].start()
-
-    @pl.loop(1, Q)
+    @pl.loop(1, Q * Y)
     def _(i):
-        greet(q_device(lax.rem(q + i, Q)))
-
-    @pl.loop(1, Y)
-    def _(i):
-        greet({"chan": lax.rem(y + i, Y)})
+        other = lax.rem(q * Y + y + i, Q * Y)
+        greet({**q_device(other // Y), "chan": lax.rem(other, Y)})
 
     @pl.when(rank > 0)
     def _():
@@ -188,7 +198,7 @@
     BEFORE = LOCAL + 2
     AFTER = LOCAL + 3
     FIELD_TAIL = LOCAL + 4
-    OUT_TAIL = LOCAL + 5
+    OUT_TAIL = FIELD_TAIL + cycles
     cut = size // 2 // TILE * TILE
 
     def forward(j):
@@ -214,18 +224,18 @@
 
         land[j, q] = buf[j, q]
 
-    copies[0].wait()
-    copies[1].wait()
-    for copy in copies[2:]:
+    for copy in copies[:FIRST]:
+        copy.wait()
+    for copy in copies[FIRST:]:
         copy.start()
     forward(0)
-    greeted = (Z - 1) + (Q - 1) + (Y - 1)
+    greeted = (Z - 1) + (Q * Y - 1)
     greeted = greeted + jnp.where(rank > 0, 1, 0) + jnp.where(rank < R - 1, 1, 0)
     pl.semaphore_wait(barrier, greeted)
     send_z(z1_send, z1_recv, 0, Z1)
 
     for j in range(1, modes):
-        copies[1 + j].wait()
+        copies[FIRST - 1 + j].wait()
         forward(j)
         send_z(z1_send, z1_recv, j, Z1)
 
@@ -255,14 +265,6 @@
         leg_t[j] = lax.dot_general(
             perm[...], basis[j].astype(BF16), (((1,), (1,)), ((), ())), preferred_element_type=F32
         ).astype(BF16)
-    for a in range(Y):
-        real = mix_all[y, 0, a * width : (a + 1) * width, :]
-        imag = mix_all[y, 1, a * width : (a + 1) * width, :]
-        at = 2 * a * width
-        mix_w[at : at + width, :width] = real
-        mix_w[at : at + width, width:] = imag
-        mix_w[at + width : at + 2 * width, :width] = -imag
-        mix_w[at + width : at + 2 * width, width:] = real
     gain = jnp.transpose(jnp.broadcast_to(gain_in[...].reshape(1, L), (width, L)))
 
     def to_owners(j):
@@ -273,11 +275,19 @@
                 x1_send[j, :, part, c] = turned[part * Q : (part + 1) * Q]
         send_q(x1_send, x1_recv, j, X1)
 
-    def send_rows(j, cut, at):
-        @pl.loop(1, Q)
-        def _(i):
-            other = lax.rem(q + i, Q)
-            send(x2_send.at[j, other, cut], x2_recv.at[j, q, cut], at + j, q_device(other))
+    def build_weights():
+        await_recv(mix_all.at[pl.ds(0, Y - 1)], MIX)
+        for b in range(Y):
+            left = slice(2 * b * width, (2 * b + 1) * width)
+            right = slice((2 * b + 1) * width, (2 * b + 2) * width)
+            for a in range(Y):
+                real = mix_all[b, 0, a * width : (a + 1) * width, :]
+                imag = mix_all[b, 1, a * width : (a + 1) * width, :]
+                at = 2 * a * width
+                mix_w[at : at + width, left] = real
+                mix_w[at : at + width, right] = imag
+                mix_w[at + width : at + 2 * width, left] = -imag
+                mix_w[at + width : at + 2 * width, right] = real
 
     def legendre(j):
         await_recv(x1_recv.at[j, pl.ds(0, Q - 1)], X1 + j)
@@ -295,33 +305,72 @@
         back = jnp.dot(leg_t[j], scaled, preferred_element_type=F32).astype(BF16)
         for part in range(2):
             piece = back[:plane, part * width : (part + 1) * width]
-            x2_send[j, :, 0, part] = piece.reshape(Q, Z, width)
-        send_rows(j, pl.ds(0, 1), X2)
-        x2_recv[j, q, 0] = x2_send[j, q, 0]
-        gathered[j, y] = back[plane:]
+            x2_send[j, :, part] = piece.reshape(Q, Z, width)
+
+        @pl.loop(1, Q)
+        def _(i):
+            other = lax.rem(q + i, Q)
+            send(x2_send.at[j, other], x2_recv.at[j, q], X2 + j, q_device(other))
+
+        x2_recv[j, q] = x2_send[j, q]
+        rows = back[plane:].reshape(cycles - 1, X, K, Z, 2 * width)
+        for a in range(Y):
+            rows_send[j, a] = rows[a // K, :, a % K]
 
         @pl.loop(1, Y)
         def _(i):
-            send(gathered.at[j, y], gathered.at[j, y], GATHER + j, {"chan": lax.rem(y + i, Y)})
+            other = lax.rem(y + i, Y)
+            send(rows_send.at[j, other], gathered.at[j, y], GATHER + j, {"chan": other})
+
+        gathered[j, y] = rows_send[j, y]
 
     def mix(j):
         await_recv(gathered.at[j, pl.ds(0, Y - 1)], GATHER + j)
-        values = jnp.concatenate([gathered[j, a] for a in range(Y)], axis=1)
+        values = jnp.concatenate(
+            [gathered[j, a].reshape(X * Z, 2 * width) for a in range(Y)], axis=1
+        )
         mixed = jnp.dot(values, mix_w[...], preferred_element_type=F32).astype(BF16)
-        for c in range(1, cycles):
+        for b in range(Y):
             for part in range(2):
-                piece = mixed[(c - 1) * plane : c * plane, part * width : (part + 1) * width]
-                x2_send[j, :, c, part] = piece.reshape(Q, Z, width)
-        send_rows(j, rest, X2_REST)
-        x2_recv[j, q, 1:] = x2_send[j, q, 1:]
+                at = (2 * b + part) * width
+                mixed_send[j, :, b, part] = mixed[:, at : at + width].reshape(X, Z, width)
+        slot = (y // K) * Q + q
+
+        @pl.loop(0, X * Y)
+        def _(n):
+            to_x = lax.rem(x + n // Y, X)
+            other = lax.rem(y + n + 1, Y)
+
+            @pl.when(jnp.logical_or(to_x * K + lax.rem(y, K) != q, other != y))
+            def _():
+                send(
+                    mixed_send.at[j, to_x, other],
+                    late_recv.at[j, slot],
+                    X2_REST + j,
+                    {"lat_0": to_x, "lat_2": lax.rem(y, K), "chan": other},
+                )
+
+        @pl.when(has_own)
+        def _():
+            late_recv[j, slot] = mixed_send[j, x, y]
+
+    def all_but_own(wait, j):
+        @pl.when(has_own)
+        def _():
+            wait(late_recv.at[j, pl.ds(0, n_late - 1)], X2_REST + j)
+
+        @pl.when(jnp.logical_not(has_own))
+        def _():
+            wait(late_recv.at[j, pl.ds(0, n_late)], X2_REST + j)
 
     def to_cycles(j, which):
         if which == [0]:
-            await_recv(x2_recv.at[j, pl.ds(0, Q - 1), 0], X2 + j)
+            await_recv(x2_recv.at[j, pl.ds(0, Q - 1)], X2 + j)
         else:
-            await_recv(x2_recv.at[j, pl.ds(0, Q - 1), rest], X2_REST + j)
+            all_but_own(await_recv, j)
         for c in which:
-            parts = [x2_recv[j, a, c, part].astype(F32) for part in range(2) for a in range(Q)]
+            land, lead = (x2_recv, 0) if c == 0 else (late_recv, (c - 1) * Q)
+            parts = [land[j, lead + a, part].astype(F32) for part in range(2) for a in range(Q)]
             z2_send[j, :, c] = jnp.swapaxes(jnp.stack(parts), 0, 1).astype(BF16)
 
             @pl.loop(0, Z - 1)
@@ -415,6 +464,7 @@
     later = list(range(1, cycles))
     to_owners(0)
     legendre(0)
+    build_weights()
     for j in range(1, modes):
         to_owners(j)
         to_cycles(j - 1, [0])
@@ -462,17 +512,14 @@
             field_recv[y] = field_send[:, pl.ds(mine, size)]
         else:
             sum_send[c - 1] = found.astype(BF16)
-            if c == cycles - 1:
-                share(sum_send.at[c - 1], sum_recv.at[c - 1], FIELD + c, 0, cut)
-                share(sum_send.at[c - 1], sum_recv.at[c - 1], FIELD_TAIL, cut, size - cut)
-            else:
-                share(sum_send.at[c - 1], sum_recv.at[c - 1], FIELD + c)
+            share(sum_send.at[c - 1], sum_recv.at[c - 1], FIELD + c, 0, cut)
+            share(sum_send.at[c - 1], sum_recv.at[c - 1], FIELD_TAIL + c, cut, size - cut)
             sum_recv[c - 1, y] = sum_send[c - 1, pl.ds(mine, size)]
 
     def perceptron(c, low=0, rows=None):
         rows = size if rows is None else rows
         own = slice(low, low + rows)
-        out_at, field_at = (OUT + c, FIELD + c) if low == 0 else (OUT_TAIL, FIELD_TAIL)
+        out_at, field_at = (OUT + c, FIELD + c) if low == 0 else (OUT_TAIL + c, FIELD_TAIL + c)
         if c == 0:
             await_recv(field_recv.at[pl.ds(0, Y - 1)], FIELD)
             points = jnp.concatenate(
@@ -531,9 +578,9 @@
                 out[c, Y * step :, :] = out_send[c, y, step:]
 
     def out_pieces(c):
-        if c < cycles - 1:
+        if c == 0:
             return [(OUT + c, step)]
-        return [(OUT + c, cut), (OUT_TAIL, step - cut)]
+        return [(OUT + c, cut), (OUT_TAIL + c, step - cut)]
 
     def finish(c):
         for at, main in out_pieces(c):
@@ -549,25 +596,23 @@
     to_points(0)
     to_cycles(last, later)
     partly(1)
-    await_recv(mix_all.at[pl.ds(0, Y - 1)], MIX)
     await_recv(local_recv.at[pl.ds(0, Y - 1)], LOCAL)
     perceptron(0)
     for c in range(1, cycles):
         if c > 1:
             partly(c)
         to_points(c)
-    for c in range(1, cycles - 1):
-        perceptron(c)
-    perceptron(cycles - 1, 0, cut)
-    perceptron(cycles - 1, cut, size - cut)
+    for c in range(1, cycles):
+        perceptron(c, 0, cut)
+        perceptron(c, cut, size - cut)
     for c in range(cycles):
         finish(c)
 
     for j in range(modes):
         await_send(z1_send.at[j, pl.ds(0, Z - 1)], Z1 + j)
         await_send(x1_send.at[j, pl.ds(0, Q - 1)], X1 + j)
-        await_send(x2_send.at[j, pl.ds(0, Q - 1), 0], X2 + j)
-        await_send(x2_send.at[j, pl.ds(0, Q - 1), rest], X2_REST + j)
+        await_send(x2_send.at[j, pl.ds(0, Q - 1)], X2 + j)
+        all_but_own(await_send, j)
         await_send(gathered.at[j, pl.ds(0, Y - 1)], GATHER + j)
     await_send(local_recv.at[pl.ds(0, Y - 1)], LOCAL)
     await_send(mix_all.at[pl.ds(0, Y - 1)], MIX)
@@ -576,11 +621,9 @@
         await_send(z2_send.at[last, pl.ds(0, Z - 1), c], LAST + c)
         if c == 0:
             await_send(field_recv.at[pl.ds(0, Y - 1)], FIELD)
-        elif c < cycles - 1:
-            await_send(sum_recv.at[c - 1, pl.ds(0, Y - 1)], FIELD + c)
         else:
             await_send(sum_recv.at[c - 1, pl.ds(0, Y - 1), pl.ds(0, cut)], FIELD + c)
-            await_send(sum_recv.at[c - 1, pl.ds(0, Y - 1), pl.ds(cut, size - cut)], FIELD_TAIL)
+            await_send(sum_recv.at[c - 1, pl.ds(0, Y - 1), pl.ds(cut, size - cut)], FIELD_TAIL + c)
         for at, main in out_pieces(c):
             await_send(out.at[c, pl.ds(0, (Y - 1) * main)], at)
 
@@ -629,10 +672,9 @@
     any_space = pl.BlockSpec(memory_space=pl.ANY)
     vmem = pl.BlockSpec(memory_space=pltpu.VMEM)
     pad = 8
-    n_sem = 5 * modes + 5 * cycles + 6
+    n_sem = 5 * modes + 7 * cycles + 4
     around_z = (modes, Z, cycles, 2 * Q, width)
     around_q = (modes, Q, 2, cycles, Z, width)
-    around_back = (modes, Q, cycles, 2, Z, width)
     scratch = [
         pltpu.VMEM((L,), F32),
         pltpu.VMEM((1, nlat), F32),
@@ -646,7 +688,7 @@
         pltpu.VMEM(perm.shape, BF16),
         pltpu.VMEM(basis.shape, F32),
         pltpu.VMEM((Y, 2, C, width), BF16),
-        pltpu.VMEM((2 * C, 2 * width), BF16),
+        pltpu.VMEM((2 * C, 2 * C), BF16),
         pltpu.VMEM(up_weight.shape, BF16),
         pltpu.VMEM(down_weight.shape, BF16),
         pltpu.VMEM((modes, L, nlat), BF16),
@@ -655,9 +697,12 @@
         pltpu.VMEM(around_z, BF16),
         pltpu.VMEM(around_q, BF16),
         pltpu.VMEM(around_q, BF16),
-        pltpu.VMEM((modes, Y, (cycles - 1) * Q * Z, 2 * width), BF16),
-        pltpu.VMEM(around_back, BF16),
-        pltpu.VMEM(around_back, BF16),
+        pltpu.VMEM((modes, Y, X, Z, 2 * width), BF16),
+        pltpu.VMEM((modes, Y, X, Z, 2 * width), BF16),
+        pltpu.VMEM((modes, X, Y, 2, Z, width), BF16),
+        pltpu.VMEM((modes, Q, 2, Z, width), BF16),
+        pltpu.VMEM((modes, Q, 2, Z, width), BF16),
+        pltpu.VMEM((modes, (cycles - 1) * Q, 2, Z, width), BF16),
         pltpu.VMEM(around_z, BF16),
         pltpu.VMEM(around_z, BF16),
         pltpu.VMEM((2, nlon, width), BF16),
@@ -671,7 +716,7 @@
         pltpu.VMEM((cycles - 1, nlon, width), BF16),
         pltpu.VMEM((cycles - 1, Y, size, width), BF16),
         pltpu.VMEM((cycles, Y, size, width), BF16),
-        pltpu.SemaphoreType.DMA((13 + modes,)),
+        pltpu.SemaphoreType.DMA((2 * cycles + modes + 15,)),
         pltpu.SemaphoreType.DMA((n_sem,)),
         pltpu.SemaphoreType.DMA((n_sem,)),
     ]

time: 85.3 us -> 84.4 us (0.989)
  the two profiles are of different devices: /device:TPU:2 before, /device:TPU:32 now
where the time goes in v5:
time: 84.4 us; the launch traced here: 84.3 us
  Pallas kernels  83.5 us (99%)
    pallas_call x1, Pallas kernels, on_device(): pl.pallas_call(functools.partial(block_kernel, dims), out_shape=pltpu.VME...  83.5 us

profile of v5, /device:TPU:32, one launch (start us, length us, event | category | flops | bytes accessed | tf_op | source)
XLA Modules:
  0.0 84.3 jit_solution(15842977010061369210)
XLA Ops:
  0.0 83.5 %block.1 = bf16[3,720,128]{2,1,0:T(8,128)(2,1)S(1)} custom-call(bf16[3,720,128]{2,1,0:T(8,128)(2,1)} %grid_in.1, bf16[3,256,720]{2,1,0:T(8,128)(2,1)} %constant.8.clone.table_in, bf16[3,720,256]{2,1,0:T(8,128)(2,1)} %constant.9.clone.inverse_in, bf16[384,384]{1,0:T(8,128)(2,1)} %constant.10.clone.perm_in, f32[3,384,384]{2,1,0:T(8,128)} %basis_in.1, ...), custom_call_target="tpu_custom_call" | custom-call | tf_op jit(solution)/shard_map/block/pallas_call | solution.py:723
  83.5 0.8 copy.16

commit v6 on v5

--- a/solution.py
+++ b/solution.py
@@ -146,10 +146,16 @@
     def greet(device):
         pl.semaphore_signal(barrier, inc=1, device_id=device, device_id_type=MESH_ID)
 
+    def far_first(own, i, length):
+        far = length - 1 - i
+        offset = jnp.where(lax.rem(far, 2) == 1, (far + 1) // 2, length - far // 2)
+        return lax.rem(own + offset, length)
+
     def ring_place(i):
-        far = Z - 1 - i
-        offset = jnp.where(lax.rem(far, 2) == 1, (far + 1) // 2, Z - far // 2)
-        return lax.rem(z + offset, Z)
+        return far_first(z, i, Z)
+
+    def q_place(i):
+        return far_first(x, i // K, X) * K + lax.rem(k + 1 + lax.rem(i, K), K)
 
     for copy in copies[:FIRST]:
         copy.start()
@@ -217,9 +223,9 @@
         land[j, z] = buf[j, z]
 
     def send_q(buf, land, j, at):
-        @pl.loop(1, Q)
+        @pl.loop(0, Q - 1)
         def _(i):
-            other = lax.rem(q + i, Q)
+            other = q_place(i)
             send(buf.at[j, other], land.at[j, q], at + j, q_device(other))
 
         land[j, q] = buf[j, q]
@@ -307,9 +313,9 @@
             piece = back[:plane, part * width : (part + 1) * width]
             x2_send[j, :, part] = piece.reshape(Q, Z, width)
 
-        @pl.loop(1, Q)
+        @pl.loop(0, Q - 1)
         def _(i):
-            other = lax.rem(q + i, Q)
+            other = q_place(i)
             send(x2_send.at[j, other], x2_recv.at[j, q], X2 + j, q_device(other))
 
         x2_recv[j, q] = x2_send[j, q]
@@ -317,9 +323,9 @@
         for a in range(Y):
             rows_send[j, a] = rows[a // K, :, a % K]
 
-        @pl.loop(1, Y)
+        @pl.loop(0, Y - 1)
         def _(i):
-            other = lax.rem(y + i, Y)
+            other = far_first(y, i, Y)
             send(rows_send.at[j, other], gathered.at[j, y], GATHER + j, {"chan": other})
 
         gathered[j, y] = rows_send[j, y]
@@ -338,8 +344,8 @@
 
         @pl.loop(0, X * Y)
         def _(n):
-            to_x = lax.rem(x + n // Y, X)
-            other = lax.rem(y + n + 1, Y)
+            to_x = far_first(x, n // Y, X)
+            other = far_first(y, lax.rem(n, Y), Y)
 
             @pl.when(jnp.logical_or(to_x * K + lax.rem(y, K) != q, other != y))
             def _():
@@ -442,9 +448,9 @@
     def share(src, dst, at, low=0, rows=None):
         rows = size if rows is None else rows
 
-        @pl.loop(1, Y)
+        @pl.loop(0, Y - 1)
         def _(i):
-            other = lax.rem(y + i, Y)
+            other = far_first(y, i, Y)
             first = pl.multiple_of(other * step, TILE) + low
             lead = (slice(None),) * (len(src.shape) - 2)
             send(
@@ -548,9 +554,9 @@
         main = min(low + rows, step) - low
         extra = low + rows > step
 
-        @pl.loop(1, Y)
+        @pl.loop(0, Y - 1)
         def _(i):
-            other = lax.rem(y + i, Y)
+            other = far_first(y, i, Y)
             send(
                 out_send.at[c, other, pl.ds(low, main)],
                 out.at[c, pl.ds(mine + low, main)],

time: 84.4 us -> 84.8 us (level)
  the two profiles are of different devices: /device:TPU:32 before, /device:TPU:8 now
where the time goes in v6:
time: 84.8 us; the launch traced here: 84.7 us
  Pallas kernels  83.9 us (99%)
    pallas_call x1, Pallas kernels, on_device(): pl.pallas_call(functools.partial(block_kernel, dims), out_shape=pltpu.VME...  83.9 us

profile of v6, /device:TPU:8, one launch (start us, length us, event | category | flops | bytes accessed | tf_op | source)
XLA Modules:
  0.0 84.7 jit_solution(13852637628922487915)
XLA Ops:
  0.0 83.9 %block.1 = bf16[3,720,128]{2,1,0:T(8,128)(2,1)S(1)} custom-call(bf16[3,720,128]{2,1,0:T(8,128)(2,1)} %grid_in.1, bf16[3,256,720]{2,1,0:T(8,128)(2,1)} %constant.8.clone.table_in, bf16[3,720,256]{2,1,0:T(8,128)(2,1)} %constant.9.clone.inverse_in, bf16[384,384]{1,0:T(8,128)(2,1)} %constant.10.clone.perm_in, f32[3,384,384]{2,1,0:T(8,128)} %basis_in.1, ...), custom_call_target="tpu_custom_call" | custom-call | tf_op jit(solution)/shard_map/block/pallas_call | solution.py:729
  83.9 0.8 copy.16
